TPU v7x, 32 devices: a whole 2x2x4 slice. The times are simulated.
32 devices in a mesh: seq: 8 (over z, y), head: 4 (over x, core).
Axes of the slice: x: 2, y: 2, z: 4, core: 2. Of those that a mesh axis runs over, the one named last changes fastest.
Arguments:
- queries: bfloat16 [8192, 2048], P('seq', 'head'), may hold values from -100 to 100
- values: bfloat16 [8192, 2048], P('seq', 'head'), may hold values from -6 to 6
- codes: int32 [8192, 16], P('seq', 'head'), may hold values from 0 to 511
- codebook: bfloat16 [16, 512, 128], P('head'), may hold values from -4 to 4
- out_weight: bfloat16 [2048, 2048], P('head'), may hold values from -0.125 to 0.125
- grad_out: bfloat16 [8192, 2048], P('seq', 'head'), may hold values from -6 to 6
Outputs:
- grad_queries: bfloat16 [8192, 2048], P('seq', 'head')
- grad_values: bfloat16 [8192, 2048], P('seq', 'head')
- grad_codebook: float32 [16, 512, 128], P('head')
All inputs are finite; a program needn't handle non-finite values.
Results may differ from a plain program's by a relative error of at most 0.012.
The roundings to bfloat16 on the way count: a program that leaves them out, or rounds other values in their place, can miss the bound.
Values may be sent and summed in bfloat16 or wider, within the bound.
A program may use at most 192 MiB of HBM per device.

v0:
```python
import functools

import jax
import jax.numpy as jnp
from jax import lax
from jax.experimental import pallas as pl
from jax.experimental.pallas import tpu as pltpu
from jax.sharding import PartitionSpec as P

BLOCK = 512
CHUNKS = 4
NEG = -1e30
F32 = jnp.float32
BF16 = jnp.bfloat16
MESH = pl.DeviceIdType.MESH


def nn(a, b):
    return lax.dot_general(a, b, (((1,), (0,)), ((), ())), preferred_element_type=F32)


def nt(a, b):
    return lax.dot_general(a, b, (((1,), (1,)), ((), ())), preferred_element_type=F32)


def kernel(
    n_seq, n_head,
    q_ref, v_ref, codes_ref, cb_ref, w_ref, go_ref,
    gq_ref, gv_ref, gc_ref,
    gath, dout, hot_t, hot, keys, keys_t, own, cnt_block, cnt_send, cnt_recv, cnt_before,
    p1_send, p1_recv, p2_send, p2_recv, local_part, vpart, s1_send, s1_recv, s2_send, s2_recv,
    ag_s, ag_r, cn_s, cn_r, p1_s, p1_r, p2_s, p2_r, s1_s, s1_r, s2_s, s2_r,
):
    rows_all = q_ref.shape[0]
    heads, entries, width = cb_ref.shape
    nb = rows_all // BLOCK
    part = entries // n_seq
    scale = width ** (-0.5)
    me = lax.axis_index("seq")
    mine = lax.axis_index("head")
    bits = []
    bit = n_head // 2
    while bit >= 1:
        bits.append(bit)
        bit //= 2

    def flip(index, mask):
        for b in bits:
            if mask & b:
                index = index + b - 2 * b * ((index // b) % 2)
        return index

    barrier = pltpu.get_barrier_semaphore()

    def greet(k, carry):
        pl.semaphore_signal(barrier, inc=1, device_id={"seq": (me + k) % n_seq}, device_id_type=MESH)
        return carry

    lax.fori_loop(1, n_seq, greet, 0)
    for b in bits:
        pl.semaphore_signal(barrier, inc=1, device_id={"head": flip(mine, b)}, device_id_type=MESH)
    pl.semaphore_wait(barrier, n_seq - 1 + len(bits))

    piece = rows_all // CHUNKS

    def gather_copy(src_mask, to, chunk):
        block = flip(mine, src_mask)
        span = pl.ds(chunk * piece, piece)
        src = go_ref.at[span] if src_mask == 0 else gath.at[block, span]
        slot = src_mask ^ to
        return pltpu.make_async_remote_copy(
            src_ref=src, dst_ref=gath.at[block, span],
            send_sem=ag_s.at[slot, chunk], recv_sem=ag_r.at[slot, chunk],
            device_id={"head": flip(mine, to)}, device_id_type=MESH)

    plan = []
    known = [0]
    for b in bits:
        plan += [(m, b) for m in known]
        known += [m ^ b for m in known]
    for m, b in plan:
        if m == 0:
            for chunk in range(CHUNKS):
                gather_copy(m, b, chunk).start()
    by_slot = {m ^ b: (m, b) for m, b in plan}
    taken = set()

    def arrive(slot, chunk):
        if (slot, chunk) not in taken:
            taken.add((slot, chunk))
            m, b = by_slot[slot]
            gather_copy(m, b, chunk).wait_recv()

    def forward(chunk):
        for m, b in plan:
            if m != 0:
                arrive(m, chunk)
                gather_copy(m, b, chunk).start()

    gath[mine] = go_ref[...]

    row_at = lax.broadcasted_iota(jnp.int32, (entries, BLOCK), 0)
    lane_at = lax.broadcasted_iota(jnp.int32, (BLOCK, entries), 1)

    def sums(h, carry):
        head_lanes = pl.ds(pl.multiple_of(h * width, width), width)
        total_values = jnp.zeros((entries, width), F32)
        total_counts = jnp.zeros((1, entries), F32)
        for b in range(nb):
            rows = pl.ds(b * BLOCK, BLOCK)
            code_row = codes_ref[h, :, rows]
            code_full = jnp.transpose(jnp.broadcast_to(code_row, (width, BLOCK)))
            code_cols = jnp.concatenate([code_full] * (entries // width), axis=1)
            one_t = (row_at == code_row).astype(F32).astype(BF16)
            one_f = (lane_at == code_cols).astype(F32)
            one = one_f.astype(BF16)
            hot_t[h, b] = one_t
            hot[h, b] = one
            key = nn(one, cb_ref[h])
            keys[h, b] = key.astype(BF16)
            keys_t[h, b] = jnp.transpose(key).astype(BF16)
            values = nn(one_t, v_ref[rows, head_lanes])
            counts = jnp.sum(one_f, axis=0, keepdims=True)
            own[h, b] = values
            cnt_block[h, b] = counts
            total_values += values
            total_counts += counts
        p1_send[:, h] = total_values.astype(BF16).reshape(n_seq, part, width)
        cnt_send[h] = total_counts
        return carry

    lax.fori_loop(0, heads, sums, 0)

    def count_copy(to, source):
        return pltpu.make_async_remote_copy(
            src_ref=cnt_send, dst_ref=cnt_recv.at[source], send_sem=cn_s.at[to], recv_sem=cn_r.at[source],
            device_id={"seq": to}, device_id_type=MESH)

    def prefix_out(to, source):
        return pltpu.make_async_remote_copy(
            src_ref=p1_send.at[to], dst_ref=p1_recv.at[source], send_sem=p1_s.at[to], recv_sem=p1_r.at[source],
            device_id={"seq": to}, device_id_type=MESH)

    def prefix_back(to, source):
        return pltpu.make_async_remote_copy(
            src_ref=p2_send.at[to], dst_ref=p2_recv.at[source], send_sem=p2_s.at[to], recv_sem=p2_r.at[source],
            device_id={"seq": to}, device_id_type=MESH)

    def over_peers(action):
        def body(k, carry):
            action((me + k) % n_seq)
            return carry

        lax.fori_loop(1, n_seq, body, 0)

    def send_sums(peer):
        prefix_out(peer, me).start()
        count_copy(peer, me).start()

    over_peers(send_sums)
    p1_recv[me] = p1_send[me]
    for chunk in range(CHUNKS // 2):
        forward(chunk)
    over_peers(lambda peer: prefix_out(peer, peer).wait_recv())

    def scan_step(j, total):
        p2_send[j] = total.astype(BF16)
        return total + p1_recv[j].astype(F32)

    lax.fori_loop(0, n_seq, scan_step, jnp.zeros((heads, part, width), F32))
    over_peers(lambda peer: prefix_back(peer, me).start())
    p2_recv[me] = p2_send[me]
    over_peers(lambda peer: count_copy(peer, peer).wait_recv())
    cnt_before[...] = lax.fori_loop(0, me, lambda j, total: total + cnt_recv[j], jnp.zeros(cnt_before.shape, F32))
    for chunk in range(CHUNKS // 2, CHUNKS):
        forward(chunk)
    for chunk in range(CHUNKS):
        for slot in by_slot:
            arrive(slot, chunk)

    depth = go_ref.shape[1]

    def project(r, carry):
        rows = pl.ds(pl.multiple_of(r * BLOCK, BLOCK), BLOCK)
        total = nt(gath[0, rows], w_ref[:, 0:depth])
        for k in range(1, n_head):
            total += nt(gath[k, rows], w_ref[:, k * depth:(k + 1) * depth])
        dout[rows] = total.astype(BF16)
        return carry

    lax.fori_loop(0, nb, project, 0)
    over_peers(lambda peer: prefix_back(peer, peer).wait_recv())

    def late_out(h, to, source):
        return pltpu.make_async_remote_copy(
            src_ref=s1_send.at[h, to], dst_ref=s1_recv.at[h, source],
            send_sem=s1_s.at[h, to], recv_sem=s1_r.at[h, source],
            device_id={"seq": to}, device_id_type=MESH)

    def late_back(h, to, source):
        return pltpu.make_async_remote_copy(
            src_ref=s2_send.at[h, to], dst_ref=s2_recv.at[h, source],
            send_sem=s2_s.at[h, to], recv_sem=s2_r.at[h, source],
            device_id={"seq": to}, device_id_type=MESH)

    def combine(h):
        over_peers(lambda peer: late_out(h, peer, peer).wait_recv())

        def code_step(j, total):
            return total + s1_recv[h, j, 1].astype(F32)

        code = lax.fori_loop(0, n_seq, code_step, jnp.zeros((part, width), F32)).astype(BF16)

        def later_step(k, total):
            j = n_seq - 1 - k
            s2_send[h, j, 0] = total.astype(BF16)
            s2_send[h, j, 1] = code
            return total + s1_recv[h, j, 0].astype(F32)

        lax.fori_loop(0, n_seq, later_step, jnp.zeros((part, width), F32))
        over_peers(lambda peer: late_back(h, peer, me).start())
        s2_recv[h, me] = s2_send[h, me]

    def attend(h, carry):
        head_lanes = pl.ds(pl.multiple_of(h * width, width), width)
        book = cb_ref[h]
        book_t = jnp.transpose(book.astype(F32)).astype(BF16)
        prefix = p2_recv[:, h].astype(F32).reshape(entries, width)
        count_row = cnt_before[h]
        code_total = jnp.zeros((entries, width), F32)
        part_total = jnp.zeros((entries, width), F32)
        for b in range(nb):
            rows = pl.ds(b * BLOCK, BLOCK)
            query = q_ref[rows, head_lanes]
            value = v_ref[rows, head_lanes]
            grad = dout[rows, head_lanes]
            key = keys[h, b]
            cache_values = prefix.astype(BF16)
            count_full = jnp.transpose(jnp.broadcast_to(count_row, (width, entries)))
            bias_full = jnp.where(count_full > 0.0, 0.0, NEG)
            counts = jnp.concatenate([count_full] * (BLOCK // width), axis=1)
            bias = jnp.concatenate([bias_full] * (BLOCK // width), axis=1)
            at_u = lax.broadcasted_iota(jnp.int32, (BLOCK, BLOCK), 0)
            at_t = lax.broadcasted_iota(jnp.int32, (BLOCK, BLOCK), 1)
            scores = jnp.where(at_u <= at_t, nt(key, query) * scale, NEG)
            cache_scores = nt(book, query) * scale + bias
            highest = jnp.maximum(
                jnp.max(scores, axis=0, keepdims=True), jnp.max(cache_scores, axis=0, keepdims=True))
            local_exp = jnp.exp(scores - highest)
            cache_exp = jnp.exp(cache_scores - highest)
            total = jnp.sum(local_exp, axis=0, keepdims=True) + jnp.sum(cache_exp * counts, axis=0, keepdims=True)
            inverse = 1.0 / total
            local_prob = local_exp * inverse
            cache_prob = cache_exp * inverse
            local_low = local_prob.astype(BF16)
            cache_low = cache_prob.astype(BF16)
            local_grad = nt(value, grad)
            cache_grad = nt(cache_values, grad)
            delta = (jnp.sum(local_low.astype(F32) * local_grad, axis=0, keepdims=True)
                     + jnp.sum(cache_low.astype(F32) * cache_grad, axis=0, keepdims=True))
            local_score_grad = (local_prob * (local_grad - delta) * scale).astype(BF16)
            cache_score_grad = (cache_prob * (cache_grad - delta * counts) * scale).astype(BF16)
            gq_t = nn(keys_t[h, b], local_score_grad) + nn(book_t, cache_score_grad)
            gq_ref[rows, head_lanes] = jnp.transpose(gq_t).astype(BF16)
            key_grad = nn(local_score_grad, query).astype(BF16)
            code_total += nn(hot_t[h, b], key_grad) + nn(cache_score_grad, query)
            value_part = nn(cache_low, grad)
            vpart[h, b] = value_part
            part_total += value_part
            local_part[h, b] = nn(local_low, grad)
            prefix = prefix + own[h, b]
            count_row = count_row + cnt_block[h, b]
        s1_send[h, :, 0] = part_total.astype(BF16).reshape(n_seq, part, width)
        s1_send[h, :, 1] = code_total.astype(BF16).reshape(n_seq, part, width)
        s1_recv[h, me] = s1_send[h, me]
        over_peers(lambda peer: late_out(h, peer, me).start())

        @pl.when(h >= 1)
        def _():
            combine(h - 1)

        return carry

    lax.fori_loop(0, heads, attend, 0)
    combine(heads - 1)

    def finish(h, carry):
        head_lanes = pl.ds(pl.multiple_of(h * width, width), width)
        over_peers(lambda peer: late_back(h, peer, peer).wait_recv())
        gc_ref[h] = s2_recv[h, :, 1].astype(F32).reshape(entries, width)
        later = s2_recv[h, :, 0].astype(F32).reshape(entries, width)
        for b in reversed(range(nb)):
            rows = pl.ds(b * BLOCK, BLOCK)
            lookup = nn(hot[h, b], later.astype(BF16))
            gv_ref[rows, head_lanes] = (local_part[h, b] + lookup).astype(BF16)
            later = later + vpart[h, b]
        over_peers(lambda peer: late_out(h, peer, me).wait_send())
        over_peers(lambda peer: late_back(h, peer, me).wait_send())
        return carry

    lax.fori_loop(0, heads, finish, 0)

    def drain(peer):
        prefix_out(peer, me).wait_send()
        prefix_back(peer, me).wait_send()
        count_copy(peer, me).wait_send()

    over_peers(drain)
    for m, b in plan:
        for chunk in range(CHUNKS):
            gather_copy(m, b, chunk).wait_send()


def per_device(queries, values, codes, codebook, out_weight, grad_out):
    n_seq, n_head = lax.axis_size("seq"), lax.axis_size("head")
    row_count = queries.shape[0]
    heads, entries, width = codebook.shape
    nb = row_count // BLOCK
    part = entries // n_seq
    codes_t = codes.T.reshape(heads, 1, row_count)
    vmem = pl.BlockSpec(memory_space=pltpu.VMEM)
    dma = pltpu.SemaphoreType.DMA
    late = pltpu.VMEM((heads, n_seq, 2, part, width), BF16)
    early = pltpu.VMEM((n_seq, heads, part, width), BF16)
    return pl.pallas_call(
        functools.partial(kernel, n_seq, n_head),
        out_shape=(
            jax.ShapeDtypeStruct(queries.shape, BF16),
            jax.ShapeDtypeStruct(queries.shape, BF16),
            jax.ShapeDtypeStruct(codebook.shape, F32),
        ),
        in_specs=[vmem] * 6,
        out_specs=(vmem,) * 3,
        scratch_shapes=[
            pltpu.VMEM((n_head,) + grad_out.shape, BF16),
            pltpu.VMEM(queries.shape, BF16),
            pltpu.VMEM((heads, nb, entries, BLOCK), BF16),
            pltpu.VMEM((heads, nb, BLOCK, entries), BF16),
            pltpu.VMEM((heads, nb, BLOCK, width), BF16),
            pltpu.VMEM((heads, nb, width, BLOCK), BF16),
            pltpu.VMEM((heads, nb, entries, width), F32),
            pltpu.VMEM((heads, nb, 1, entries), F32),
            pltpu.VMEM((heads, 1, entries), F32),
            pltpu.VMEM((n_seq, heads, 1, entries), F32),
            pltpu.VMEM((heads, 1, entries), F32),
            early, early, early, early,
            pltpu.VMEM((heads, nb, BLOCK, width), F32),
            pltpu.VMEM((heads, nb, entries, width), F32),
            late, late, late, late,
            dma((n_head, CHUNKS)), dma((n_head, CHUNKS)),
            dma((n_seq,)), dma((n_seq,)),
            dma((n_seq,)), dma((n_seq,)),
            dma((n_seq,)), dma((n_seq,)),
            dma((heads, n_seq)), dma((heads, n_seq)),
            dma((heads, n_seq)), dma((heads, n_seq)),
        ],
        compiler_params=pltpu.CompilerParams(
            collective_id=0, has_side_effects=True, vmem_limit_bytes=60 * 1024 * 1024),
    )(queries, values, codes_t, codebook, out_weight, grad_out)


def solution(mesh):
    return jax.shard_map(
        per_device,
        mesh=mesh,
        in_specs=(
            P("seq", "head"),
            P("seq", "head"),
            P("seq", "head"),
            P("head", None, None),
            P("head", None),
            P("seq", "head"),
        ),
        out_specs=(P("seq", "head"), P("seq", "head"), P("head", None, None)),
        check_vma=False,
    )
```

profile of v0, /device:TPU:0, one launch (start us, length us, event | category | flops | bytes accessed | tf_op | source)
XLA Modules:
  0.0 99.6 jit_solution(1526587193798404922)
XLA Ops:
  0.6 1.3 %reshape.9.codes_ref = s32[4,1,1024]{2,1,0:T(1,128)} reshape(s32[4,1024]{1,0:T(4,128)} %bitcast.1) | data formatting | bytes 32768 | tf_op jit(solution)/shard_map/reshape | solution.py:320
  2.0 93.3 %shard_map.85 = (bf16[1024,512]{1,0:T(8,128)(2,1)}, bf16[1024,512]{1,0:T(8,128)(2,1)}, f32[4,512,128]{2,1,0:T(8,128)}) custom-call(bf16[1024,512]{1,0:T(8,128)(2,1)} %q_ref.1, bf16[1024,512]{1,0:T(8,128)(2,1)} %v_ref.1, s32[4,1,1024]{2,1,0:T(1,128)} %reshape.9.codes_ref, bf16[4,512,128]{2,1,0:T(8,128)(2,1)} %cb_ref.1, bf16[512,2048]{1,0:T(8,128)(2,1)} %w_ref.1, ...), custom_call_target="tpu_custom_call" | custom-call | tf_op jit(solution)/shard_map/pallas_call | solution.py:325
  95.3 0.0 copy-start.1
  95.3 0.0 copy-start
  95.3 2.4 %copy.12 = bf16[1024,512]{1,0:T(8,128)(2,1)} copy(bf16[1024,512]{1,0:T(8,128)(2,1)} %get-tuple-element.6) | data formatting | bytes 2097152
  97.7 0.0 copy-done.1
  97.7 1.0 copy.13
  98.7 0.0 copy-done
  98.7 1.0 copy.14
Async XLA Ops:
  95.3 2.4 %copy-start.1 = (bf16[1024,512]{1,0:T(8,128)(2,1)S(1)}, bf16[1024,512]{1,0:T(8,128)(2,1)}, u32[]{:S(2)}) copy-start(bf16[1024,512]{1,0:T(8,128)(2,1)} %get-tuple-element.7) | copy-start | bytes 3145732
  95.3 3.4 %copy-start = (f32[4,512,128]{2,1,0:T(8,128)S(1)}, f32[4,512,128]{2,1,0:T(8,128)}, u32[]{:S(2)}) copy-start(f32[4,512,128]{2,1,0:T(8,128)} %get-tuple-element.8) | copy-start | bytes 3145732
where the time goes:
time: 99.9 us; the launch traced here: 99.6 us
  Pallas kernels  93.3 us (93%)
  local copies, waits for them, and re-layouts  5.69 us (6%)
    pallas_call x1, Pallas kernels, per_device(): pl.pallas_call(functools.partial(kernel, n_seq, n_head), out_shape=(jax.S...  93.3 us
    unnamed x7, local copies, waits for them, and re-layouts  4.36 us

commit v1 on v0

v1 whole, which is shorter than its diff:
```python
import functools

import jax
import jax.numpy as jnp
from jax import lax
from jax.experimental import pallas as pl
from jax.experimental.pallas import tpu as pltpu
from jax.sharding import PartitionSpec as P

BLOCK = 512
TILE = 256
CHUNK = 128
NEG = -1e30
LOG2E = 1.4426950408889634
F32 = jnp.float32
BF16 = jnp.bfloat16
MESH = pl.DeviceIdType.MESH


def nn(a, b):
    return lax.dot_general(a, b, (((1,), (0,)), ((), ())), preferred_element_type=F32)


def nt(a, b):
    return lax.dot_general(a, b, (((1,), (1,)), ((), ())), preferred_element_type=F32)


def kernel(
    n_seq, n_head,
    q_in, v_in, codes_in, cb_in, w_in, go_in,
    gq_ref, gv_ref, gc_ref,
    q_ref, v_ref, codes_ref, cb_ref, w_ref, gath, dout,
    hot_t, hot, keys, keys_t, book_t, own, cnt_block, cnt_pre, cnt_full, cval,
    lprob, cprob, key_acc, local_part, vpart, code_acc, later_ref,
    cn_own, cny_in, cnz_out, cnz_in,
    py_out, py_in, pz_out, pz_in, pa_out, pa_in,
    ly_out, ly_in, lz_out, lz_in, la_out, la_in,
    cy_out, cy_in, cz_out, cz_in, c_fin,
    load_s, go_s, ag_s, ag_r, cny_s, cny_r, cnz_s, cnz_r,
    py_s, py_r, pz_s, pz_r, pa_s, pa_r,
    ly_s, ly_r, lz_s, lz_r, la_s, la_r,
    cy_s, cy_r, ca_s, ca_r, cz_s, cz_r, cf_s, cf_r,
):
    rows_all = q_ref.shape[0]
    heads, entries, width = cb_ref.shape
    nb = rows_all // BLOCK
    parts = BLOCK // TILE
    chunks = rows_all // CHUNK
    per_tile = TILE // CHUNK
    outer = n_seq // 2
    half = entries // 2
    piece = half // outer
    scale = width ** (-0.5)
    me = lax.axis_index("seq")
    mine = lax.axis_index("head")
    at = me // 2
    side = me % 2
    partner = me + 1 - 2 * side
    is_hi = side.astype(F32)
    is_lo = 1.0 - is_hi
    own_half = pl.ds(pl.multiple_of(side * half, half), half)
    other_half = pl.ds(pl.multiple_of((1 - side) * half, half), half)
    has_down = at > 0
    has_up = at < outer - 1
    bits = []
    bit = n_head // 2
    while bit >= 1:
        bits.append(bit)
        bit //= 2

    def flip(index, mask):
        for b in bits:
            if mask & b:
                index = index + b - 2 * b * ((index // b) % 2)
        return index

    def go_load(chunk):
        span = pl.ds(chunk * CHUNK, CHUNK)
        return pltpu.make_async_copy(go_in.at[span], gath.at[mine, span], go_s.at[chunk])

    loads = [
        pltpu.make_async_copy(src, dst, load_s.at[k])
        for k, (src, dst) in enumerate(
            ((codes_in, codes_ref), (cb_in, cb_ref), (v_in, v_ref), (q_in, q_ref), (w_in, w_ref)))
    ]
    loads[0].start()
    for chunk in range(chunks):
        go_load(chunk).start()
    for copy in loads[1:]:
        copy.start()

    barrier = pltpu.get_barrier_semaphore()
    pl.semaphore_signal(barrier, inc=1, device_id={"seq": partner}, device_id_type=MESH)
    for b in bits:
        pl.semaphore_signal(barrier, inc=1, device_id={"head": flip(mine, b)}, device_id_type=MESH)

    def greet(k, carry):
        pl.semaphore_signal(barrier, inc=1, device_id={"seq": (me + 2 * k) % n_seq}, device_id_type=MESH)
        return carry

    lax.fori_loop(1, outer, greet, 0)
    pl.semaphore_wait(barrier, outer + len(bits))

    def gather_copy(src_mask, to, chunk):
        block = flip(mine, src_mask)
        span = pl.ds(chunk * CHUNK, CHUNK)
        slot = src_mask ^ to
        return pltpu.make_async_remote_copy(
            src_ref=gath.at[block, span], dst_ref=gath.at[block, span],
            send_sem=ag_s.at[slot, chunk], recv_sem=ag_r.at[slot, chunk],
            device_id={"head": flip(mine, to)}, device_id_type=MESH)

    plan = []
    known = [0]
    for b in bits:
        plan += [(m, b) for m in known]
        known += [m ^ b for m in known]
    by_slot = {m ^ b: (m, b) for m, b in plan}
    for chunk in range(chunks):
        go_load(chunk).wait()
        for m, b in plan:
            if m == 0 and b == bits[0]:
                gather_copy(m, b, chunk).start()
    for m, b in plan:
        if m == 0 and b != bits[0]:
            for chunk in range(chunks):
                gather_copy(m, b, chunk).start()
    taken = set()

    def arrive(slot, chunk):
        if (slot, chunk) not in taken:
            taken.add((slot, chunk))
            m, b = by_slot[slot]
            gather_copy(m, b, chunk).wait_recv()

    def relay(chunk):
        for m, b in plan:
            if m != 0:
                arrive(m, chunk)
                gather_copy(m, b, chunk).start()

    def seq_copy(src, dst, send, recv, to):
        return pltpu.make_async_remote_copy(
            src_ref=src, dst_ref=dst, send_sem=send, recv_sem=recv,
            device_id={"seq": to}, device_id_type=MESH)

    count_pair = seq_copy(cn_own, cny_in, cny_s.at[0], cny_r.at[0], partner)

    def count_chain(to):
        return seq_copy(cnz_out, cnz_in, cnz_s.at[0], cnz_r.at[0], to)

    loads[0].wait()
    row_at = lax.broadcasted_iota(jnp.int32, (entries, BLOCK), 0)
    lane_at = lax.broadcasted_iota(jnp.int32, (BLOCK, entries), 1)

    def count(h, carry):
        total = jnp.zeros((1, entries), F32)
        for b in range(nb):
            code_row = codes_ref[pl.ds(h, 1), pl.ds(b * BLOCK, BLOCK)]
            code_full = jnp.transpose(jnp.broadcast_to(code_row, (width, BLOCK)))
            code_cols = jnp.concatenate([code_full] * (entries // width), axis=1)
            one_f = (lane_at == code_cols).astype(F32)
            hot[h, b] = one_f.astype(BF16)
            counts = jnp.sum(one_f, axis=0, keepdims=True)
            cnt_block[h, b] = counts
            total += counts
        cn_own[h] = total
        return carry

    lax.fori_loop(0, heads, count, 0)
    count_pair.start()

    def share_counts():
        count_pair.wait_recv()

        @pl.when(jnp.logical_not(has_down))
        def _():
            cnz_in[...] = jnp.zeros(cnz_in.shape, F32)

        @pl.when(has_down)
        def _():
            count_chain(me - 2).wait_recv()

        cnz_out[...] = cnz_in[...] + cn_own[...] + cny_in[...]

        @pl.when(has_up)
        def _():
            count_chain(me + 2).start()

        def per_head(h, carry):
            row = cnz_in[h] + cny_in[h] * is_hi
            for b in range(nb):
                cnt_pre[h, b] = row
                row = row + cnt_block[h, b]
            return carry

        lax.fori_loop(0, heads, per_head, 0)

    def prefix_pair(h):
        return seq_copy(py_out.at[h], py_in.at[h], py_s.at[h], py_r.at[h], partner)

    def prefix_hop(h, to):
        return seq_copy(pz_out.at[h], pz_in.at[h], pz_s.at[h], pz_r.at[h], to)

    def prefix_back(h):
        return seq_copy(pa_out.at[h], pa_in.at[h], pa_s.at[h], pa_r.at[h], partner)

    loads[1].wait()
    loads[2].wait()

    def sums(h, carry):
        head_lanes = pl.ds(pl.multiple_of(h * width, width), width)
        book = cb_ref[h]
        book_t[h] = jnp.transpose(book.astype(F32)).astype(BF16)
        for b in range(nb):
            rows = pl.ds(b * BLOCK, BLOCK)
            code_row = codes_ref[pl.ds(h, 1), rows]
            one_t = (row_at == code_row).astype(F32).astype(BF16)
            hot_t[h, b] = one_t
            key = nn(hot[h, b], book)
            keys[h, b] = key.astype(BF16)
            keys_t[h, b] = jnp.transpose(key).astype(BF16)
            own[h, b] = nn(one_t, v_ref[rows, head_lanes])
        total = own[h, 0, other_half]
        for b in range(1, nb):
            total += own[h, b, other_half]
        py_out[h] = total.astype(BF16)
        prefix_pair(h).start()

        @pl.when(h == jnp.minimum(at, heads - 1))
        def _():
            share_counts()

        return carry

    lax.fori_loop(0, heads, sums, 0)

    def prefix_chain(h):
        prefix_pair(h).wait_recv()

        @pl.when(jnp.logical_not(has_down))
        def _():
            pz_in[h] = jnp.zeros(pz_in.shape[1:], BF16)

        @pl.when(has_down)
        def _():
            prefix_hop(h, me - 2).wait_recv()

        below = pz_in[h].astype(F32)
        pair = py_in[h].astype(F32)
        total = own[h, 0, own_half]
        for b in range(1, nb):
            total += own[h, b, own_half]
        pz_out[h] = (below + total + pair).astype(BF16)

        @pl.when(has_up)
        def _():
            prefix_hop(h, me + 2).start()

        pa_out[h] = (below + total * is_lo).astype(BF16)
        prefix_back(h).start()
        prefix = below + pair * is_hi
        for b in range(nb):
            cval[h, b, own_half] = prefix.astype(BF16)
            prefix = prefix + own[h, b, own_half]

    def prefix_gather(h):
        prefix_back(h).wait_recv()
        prefix = pa_in[h].astype(F32)
        for b in range(nb):
            cval[h, b, other_half] = prefix.astype(BF16)
            prefix = prefix + own[h, b, other_half]

    def softmax(h, b):
        head_lanes = pl.ds(pl.multiple_of(h * width, width), width)
        book = cb_ref[h]
        count_full = jnp.transpose(jnp.broadcast_to(cnt_pre[h, b], (width, entries)))
        cnt_full[h, b] = count_full
        bias_full = jnp.where(count_full > 0.0, 0.0, NEG)
        counts = jnp.concatenate([count_full] * (TILE // width), axis=1)
        bias = jnp.concatenate([bias_full] * (TILE // width), axis=1)
        for p in range(parts):
            seen = (p + 1) * TILE
            query = q_ref[pl.ds(pl.multiple_of(b * BLOCK + p * TILE, TILE), TILE), head_lanes]
            at_u = lax.broadcasted_iota(jnp.int32, (seen, TILE), 0)
            at_t = lax.broadcasted_iota(jnp.int32, (seen, TILE), 1) + p * TILE
            scores = jnp.where(at_u <= at_t, nt(keys[h, b, 0:seen], query) * (scale * LOG2E), NEG)
            cache_scores = nt(book, query) * (scale * LOG2E) + bias
            highest = jnp.maximum(
                jnp.max(scores, axis=0, keepdims=True), jnp.max(cache_scores, axis=0, keepdims=True))
            local_exp = jnp.exp2(scores - highest)
            cache_exp = jnp.exp2(cache_scores - highest)
            total = jnp.sum(local_exp, axis=0, keepdims=True) + jnp.sum(cache_exp * counts, axis=0, keepdims=True)
            inverse = 1.0 / total
            lprob[h, b, seen * p // 2:seen * p // 2 + seen] = local_exp * inverse
            cprob[h, b, p] = cache_exp * inverse

    loads[3].wait()
    units = heads * nb
    early = list(range(chunks // 2))
    relay(early[0])
    relay_at = {}
    for j in early[1:]:
        relay_at.setdefault(max(0, units * j // len(early) - 1), []).append(j)

    def unit(u, carry):
        h, b = u // nb, u % nb
        softmax(h, b)

        @pl.when(u < heads)
        def _():
            prefix_chain(u)

        if units >= 2 * heads:
            @pl.when((u >= heads) & (u < 2 * heads))
            def _():
                prefix_gather(u - heads)

        for step, which in relay_at.items():
            @pl.when(u == step)
            def _(which=which):
                for chunk in which:
                    relay(chunk)

        return carry

    lax.fori_loop(0, units, unit, 0)
    if units < 2 * heads:
        for h in range(heads):
            prefix_gather(h)
    loads[4].wait()

    depth = go_in.shape[1]

    def project(start):
        rows = pl.ds(start, TILE)
        total = nt(gath[0, rows], w_ref[:, 0:depth])
        for k in range(1, n_head):
            total += nt(gath[k, rows], w_ref[:, k * depth:(k + 1) * depth])
        dout[rows] = total.astype(BF16)

    def value_pass(h, b, p):
        head_lanes = pl.ds(pl.multiple_of(h * width, width), width)
        grad = dout[pl.ds(b * BLOCK + p * TILE, TILE), head_lanes]
        value = nn(cprob[h, b, p].astype(BF16), grad)
        if p == 0:
            vpart[h, b] = value
        else:
            vpart[h, b] += value

    def grad_pass(h, b, p):
        head_lanes = pl.ds(pl.multiple_of(h * width, width), width)
        rows = pl.ds(b * BLOCK + p * TILE, TILE)
        seen = (p + 1) * TILE
        query = q_ref[rows, head_lanes]
        grad = dout[rows, head_lanes]
        counts = jnp.concatenate([cnt_full[h, b]] * (TILE // width), axis=1)
        local_grad = nt(v_ref[pl.ds(b * BLOCK, seen), head_lanes], grad)
        cache_grad = nt(cval[h, b], grad)
        local_prob = lprob[h, b, seen * p // 2:seen * p // 2 + seen]
        cache_prob = cprob[h, b, p]
        local_low = local_prob.astype(BF16)
        cache_low = cache_prob.astype(BF16)
        delta = (jnp.sum(local_low.astype(F32) * local_grad, axis=0, keepdims=True)
                 + jnp.sum(cache_low.astype(F32) * cache_grad, axis=0, keepdims=True))
        local_score_grad = (local_prob * (local_grad - delta) * scale).astype(BF16)
        cache_score_grad = (cache_prob * (cache_grad - delta * counts) * scale).astype(BF16)
        gq_t = nn(keys_t[h, b, :, 0:seen], local_score_grad) + nn(book_t[h], cache_score_grad)
        gq_ref[rows, head_lanes] = jnp.transpose(gq_t).astype(BF16)
        code = nn(cache_score_grad, query)
        key_grad = nn(local_score_grad, query)
        local = nn(local_low, grad)
        last = p * TILE
        if p > 0:
            key_acc[h, 0:last] += key_grad[0:last]
            local_part[h, b, 0:last] += local[0:last]
        key_acc[h, last:seen] = key_grad[last:seen]
        local_part[h, b, last:seen] = local[last:seen]
        if p == parts - 1:
            code += nn(hot_t[h, b], key_acc[h].astype(BF16))
        if b == 0 and p == 0:
            code_acc[h] = code
        else:
            code_acc[h] += code

    def later_pair(h):
        return seq_copy(ly_out.at[h], ly_in.at[h], ly_s.at[h], ly_r.at[h], partner)

    def later_hop(h, to):
        return seq_copy(lz_out.at[h], lz_in.at[h], lz_s.at[h], lz_r.at[h], to)

    def later_back(h):
        return seq_copy(la_out.at[h], la_in.at[h], la_s.at[h], la_r.at[h], partner)

    def part_total(h, span):
        total = vpart[h, 0, span]
        for b in range(1, nb):
            total += vpart[h, b, span]
        return total

    def send_later(h):
        ly_out[h] = part_total(h, other_half).astype(BF16)
        later_pair(h).start()

    def later_chain(h):
        later_pair(h).wait_recv()

        @pl.when(jnp.logical_not(has_up))
        def _():
            lz_in[h] = jnp.zeros(lz_in.shape[1:], BF16)

        @pl.when(has_up)
        def _():
            later_hop(h, me + 2).wait_recv()

        above = lz_in[h].astype(F32)
        pair = ly_in[h].astype(F32)
        total = part_total(h, own_half)
        lz_out[h] = (above + total + pair).astype(BF16)

        @pl.when(has_down)
        def _():
            later_hop(h, me - 2).start()

        la_out[h] = (above + total * is_hi).astype(BF16)
        later_back(h).start()
        later_ref[h, own_half] = above + pair * is_lo

    def later_gather(h):
        later_back(h).wait_recv()
        later_ref[h, other_half] = la_in[h].astype(F32)
        head_lanes = pl.ds(pl.multiple_of(h * width, width), width)
        later = later_ref[h]
        for b in reversed(range(nb)):
            rows = pl.ds(b * BLOCK, BLOCK)
            lookup = nn(hot[h, b], later.astype(BF16))
            gv_ref[rows, head_lanes] = (local_part[h, b] + lookup).astype(BF16)
            later = later + vpart[h, b]

    def code_pair(h):
        return seq_copy(cy_out.at[h], cy_in.at[h], cy_s.at[h], cy_r.at[h], partner)

    def code_out(h, to, source):
        return seq_copy(
            cz_out.at[h, to], cz_in.at[h, source], cz_s.at[h, to], cz_r.at[h, source], 2 * to + side)

    def code_back(h, to, source):
        return seq_copy(
            c_fin.at[h, side, source], c_fin.at[h, side, source], cf_s.at[h, to], cf_r.at[h, source], 2 * to + side)

    def code_half(h, which):
        return seq_copy(c_fin.at[h, which], c_fin.at[h, which], ca_s.at[h], ca_r.at[h], partner)

    def over_chain(action):
        def body(k, carry):
            action((at + k) % outer)
            return carry

        lax.fori_loop(1, outer, body, 0)

    def send_code(h):
        cy_out[h] = code_acc[h, other_half].astype(BF16)
        code_pair(h).start()

    def reduce_code(h):
        code_pair(h).wait_recv()
        total = code_acc[h, own_half] + cy_in[h].astype(F32)
        cz_out[h] = total.astype(BF16).reshape(outer, piece, width)
        over_chain(lambda to: code_out(h, to, at).start())
        cz_in[h, at] = cz_out[h, at]

    def spread_code(h):
        over_chain(lambda source: code_out(h, source, source).wait_recv())
        total = cz_in[h, 0].astype(F32)
        for k in range(1, outer):
            total += cz_in[h, k].astype(F32)
        c_fin[h, side, at] = total.astype(BF16)
        over_chain(lambda to: code_back(h, to, at).start())

    def pair_code(h):
        over_chain(lambda source: code_back(h, source, source).wait_recv())
        code_half(h, side).start()
        gc_ref[h, own_half] = c_fin[h, side].astype(F32).reshape(half, width)

    def last_code(h):
        code_half(h, 1 - side).wait_recv()
        gc_ref[h, other_half] = c_fin[h, 1 - side].astype(F32).reshape(half, width)

    tiles = nb * parts
    slots = max(1, (tiles - 1) * heads)
    late = list(range(chunks // 2, chunks))
    late_at = {}
    for j, chunk in enumerate(late):
        late_at.setdefault(min(slots - 1, slots * j // len(late) + 1), []).append(chunk)

    for g in range(tiles):
        b, p = g // parts, g % parts
        final = g == tiles - 1
        if final:
            for chunk in late:
                for m, _ in plan:
                    if m != 0 and (m, chunk) not in taken:
                        relay(chunk)
        for chunk in range(g * per_tile, (g + 1) * per_tile):
            for slot in by_slot:
                arrive(slot, chunk)
        project(g * TILE)

        def values(h, carry, b=b, p=p, final=final):
            value_pass(h, b, p)
            if final:
                send_later(h)
            return carry

        lax.fori_loop(0, heads, values, 0)

        def grads(h, carry, g=g, b=b, p=p, final=final):
            grad_pass(h, b, p)
            for slot, which in late_at.items():
                if slot // heads == g:
                    @pl.when(h == slot % heads)
                    def _(which=which):
                        for chunk in which:
                            relay(chunk)
            if final:
                send_code(h)

                @pl.when(jnp.logical_not(has_up) & (h >= 1))
                def _():
                    later_chain(h - 1)

            return carry

        lax.fori_loop(0, heads, grads, 0)

    behind = outer - 1 - at
    soon = behind * 2 < outer
    last_ones = behind * 4 >= 3 * outer

    def reduce_step(h, carry):
        @pl.when(soon & (has_up | (h == heads - 1)))
        def _():
            later_chain(h)

        reduce_code(h)

        @pl.when(jnp.logical_not(soon | last_ones))
        def _():
            later_chain(h)

        return carry

    lax.fori_loop(0, heads, reduce_step, 0)

    def spread_step(h, carry):
        spread_code(h)

        @pl.when(last_ones)
        def _():
            later_chain(h)

        return carry

    lax.fori_loop(0, heads, spread_step, 0)

    def pair_step(h, carry):
        pair_code(h)
        later_gather(h)
        return carry

    lax.fori_loop(0, heads, pair_step, 0)

    def last_step(h, carry):
        last_code(h)
        return carry

    lax.fori_loop(0, heads, last_step, 0)

    def drain(h, carry):
        prefix_pair(h).wait_send()
        prefix_back(h).wait_send()
        later_pair(h).wait_send()
        later_back(h).wait_send()

        @pl.when(has_up)
        def _():
            prefix_hop(h, me + 2).wait_send()

        @pl.when(has_down)
        def _():
            later_hop(h, me - 2).wait_send()

        code_pair(h).wait_send()
        code_half(h, side).wait_send()
        over_chain(lambda to: code_out(h, to, at).wait_send())
        over_chain(lambda to: code_back(h, to, at).wait_send())
        return carry

    lax.fori_loop(0, heads, drain, 0)
    count_pair.wait_send()

    @pl.when(has_up)
    def _():
        count_chain(me + 2).wait_send()

    for m, b in plan:
        for chunk in range(chunks):
            gather_copy(m, b, chunk).wait_send()


def per_device(queries, values, codes, codebook, out_weight, grad_out):
    n_seq, n_head = lax.axis_size("seq"), lax.axis_size("head")
    row_count = queries.shape[0]
    heads, entries, width = codebook.shape
    nb = row_count // BLOCK
    parts = BLOCK // TILE
    chunks = row_count // CHUNK
    half = entries // 2
    hbm = pl.BlockSpec(memory_space=pltpu.HBM)
    vmem = pl.BlockSpec(memory_space=pltpu.VMEM)
    dma = pltpu.SemaphoreType.DMA
    halves = pltpu.VMEM((heads, half, width), BF16)
    pieces = pltpu.VMEM((heads, n_seq // 2, entries // n_seq, width), BF16)
    counts = pltpu.VMEM((heads, 1, entries), F32)
    return pl.pallas_call(
        functools.partial(kernel, n_seq, n_head),
        out_shape=(
            jax.ShapeDtypeStruct(queries.shape, BF16),
            jax.ShapeDtypeStruct(queries.shape, BF16),
            jax.ShapeDtypeStruct(codebook.shape, F32),
        ),
        in_specs=[hbm] * 6,
        out_specs=(vmem,) * 3,
        scratch_shapes=[
            pltpu.VMEM(queries.shape, BF16),
            pltpu.VMEM(queries.shape, BF16),
            pltpu.VMEM((heads, row_count), jnp.int32),
            pltpu.VMEM(codebook.shape, BF16),
            pltpu.VMEM(out_weight.shape, BF16),
            pltpu.VMEM((n_head,) + grad_out.shape, BF16),
            pltpu.VMEM(queries.shape, BF16),
            pltpu.VMEM((heads, nb, entries, BLOCK), BF16),
            pltpu.VMEM((heads, nb, BLOCK, entries), BF16),
            pltpu.VMEM((heads, nb, BLOCK, width), BF16),
            pltpu.VMEM((heads, nb, width, BLOCK), BF16),
            pltpu.VMEM((heads, width, entries), BF16),
            pltpu.VMEM((heads, nb, entries, width), F32),
            pltpu.VMEM((heads, nb, 1, entries), F32),
            pltpu.VMEM((heads, nb, 1, entries), F32),
            pltpu.VMEM((heads, nb, entries, width), F32),
            pltpu.VMEM((heads, nb, entries, width), BF16),
            pltpu.VMEM((heads, nb, (parts + 1) * BLOCK // 2, TILE), F32),
            pltpu.VMEM((heads, nb, parts, entries, TILE), F32),
            pltpu.VMEM((heads, BLOCK, width), F32),
            pltpu.VMEM((heads, nb, BLOCK, width), F32),
            pltpu.VMEM((heads, nb, entries, width), F32),
            pltpu.VMEM((heads, entries, width), F32),
            pltpu.VMEM((heads, entries, width), F32),
            counts, counts, counts, counts,
            halves, halves, halves, halves, halves, halves,
            halves, halves, halves, halves, halves, halves,
            halves, halves, pieces, pieces,
            pltpu.VMEM((heads, 2, n_seq // 2, entries // n_seq, width), BF16),
            dma((5,)), dma((chunks,)),
            dma((n_head, chunks)), dma((n_head, chunks)),
            dma((1,)), dma((1,)), dma((1,)), dma((1,)),
        ] + [dma((heads,))] * 16 + [dma((heads, n_seq // 2))] * 4,
        compiler_params=pltpu.CompilerParams(
            collective_id=0, has_side_effects=True, vmem_limit_bytes=57 * 1024 * 1024),
    )(queries, values, codes.T, codebook, out_weight, grad_out)


def solution(mesh):
    return jax.shard_map(
        per_device,
        mesh=mesh,
        in_specs=(
            P("seq", "head"),
            P("seq", "head"),
            P("seq", "head"),
            P("head", None, None),
            P("head", None),
            P("seq", "head"),
        ),
        out_specs=(P("seq", "head"), P("seq", "head"), P("head", None, None)),
        check_vma=False,
    )
```

time: 99.9 us -> 91 us (0.911)
  Pallas kernels: 93.3 us -> 85.8 us
  local copies, waits for them, and re-layouts: 5.69 us -> 4.36 us
    pallas_call x1, Pallas kernels: 93.3 us -> 85.8 us  [per_device(): pl.pallas_call(functools.partial(kernel, n_seq, n_head), out_shape=(jax.S...]
    reshape x1 -> x0, local copies, waits for them, and re-layouts: 1.33 us -> none  [per_device(): codes_t = codes.T.reshape(heads, 1, row_count)]
where the time goes in v1:
time: 91 us; the launch traced here: 90.8 us
  Pallas kernels  85.8 us (94%)
  local copies, waits for them, and re-layouts  4.36 us (5%)
    pallas_call x1, Pallas kernels, per_device(): pl.pallas_call(functools.partial(kernel, n_seq, n_head), out_shape=(jax.S...  85.8 us
    unnamed x7, local copies, waits for them, and re-layouts  4.36 us

profile of v1, /device:TPU:0, one launch (start us, length us, event | category | flops | bytes accessed | tf_op | source)
XLA Modules:
  0.0 90.8 jit_solution(2866684218666557114)
XLA Ops:
  0.6 85.8 %shard_map.85 = (bf16[1024,512]{1,0:T(8,128)(2,1)}, bf16[1024,512]{1,0:T(8,128)(2,1)}, f32[4,512,128]{2,1,0:T(8,128)}) custom-call(bf16[1024,512]{1,0:T(8,128)(2,1)} %q_in.1, bf16[1024,512]{1,0:T(8,128)(2,1)} %v_in.1, s32[4,1024]{1,0:T(4,128)} %bitcast.1, bf16[4,512,128]{2,1,0:T(8,128)(2,1)} %cb_in.1, bf16[512,2048]{1,0:T(8,128)(2,1)} %w_in.1, ...), custom_call_target="tpu_custom_call" | custom-call | tf_op jit(solution)/shard_map/pallas_call | solution.py:625
  86.4 0.0 copy-start.1
  86.5 0.0 copy-start
  86.5 2.4 %copy.12 = bf16[1024,512]{1,0:T(8,128)(2,1)} copy(bf16[1024,512]{1,0:T(8,128)(2,1)} %get-tuple-element.6) | data formatting | bytes 2097152
  88.9 0.0 copy-done.1
  88.9 1.0 %copy.13 = bf16[1024,512]{1,0:T(8,128)(2,1)} copy(bf16[1024,512]{1,0:T(8,128)(2,1)S(1)} %copy-done.1) | data formatting | bytes 2097152
  89.8 0.0 copy-done
  89.9 1.0 %copy.14 = f32[4,512,128]{2,1,0:T(8,128)} copy(f32[4,512,128]{2,1,0:T(8,128)S(1)} %copy-done) | data formatting | bytes 2097152
Async XLA Ops:
  86.4 2.4 %copy-start.1 = (bf16[1024,512]{1,0:T(8,128)(2,1)S(1)}, bf16[1024,512]{1,0:T(8,128)(2,1)}, u32[]{:S(2)}) copy-start(bf16[1024,512]{1,0:T(8,128)(2,1)} %get-tuple-element.7) | copy-start | bytes 3145732
  86.5 3.4 %copy-start = (f32[4,512,128]{2,1,0:T(8,128)S(1)}, f32[4,512,128]{2,1,0:T(8,128)}, u32[]{:S(2)}) copy-start(f32[4,512,128]{2,1,0:T(8,128)} %get-tuple-element.8) | copy-start | bytes 3145732

commit v2 on v1

--- a/solution.py
+++ b/solution.py
@@ -31,12 +31,12 @@
     gq_ref, gv_ref, gc_ref,
     q_ref, v_ref, codes_ref, cb_ref, w_ref, gath, dout,
     hot_t, hot, keys, keys_t, book_t, own, cnt_block, cnt_pre, cnt_full, cval,
-    lprob, cprob, key_acc, local_part, vpart, code_acc, later_ref,
-    cn_own, cny_in, cnz_out, cnz_in,
+    local_low, cache_low, local_part, vpart, code_acc, later_ref,
+    cn_own, cn_in,
     py_out, py_in, pz_out, pz_in, pa_out, pa_in,
     ly_out, ly_in, lz_out, lz_in, la_out, la_in,
     cy_out, cy_in, cz_out, cz_in, c_fin,
-    load_s, go_s, ag_s, ag_r, cny_s, cny_r, cnz_s, cnz_r,
+    load_s, go_s, ag_s, ag_r, cn_s, cn_r,
     py_s, py_r, pz_s, pz_r, pa_s, pa_r,
     ly_s, ly_r, lz_s, lz_r, la_s, la_r,
     cy_s, cy_r, ca_s, ca_r, cz_s, cz_r, cf_s, cf_r,
@@ -90,16 +90,34 @@
         copy.start()
 
     barrier = pltpu.get_barrier_semaphore()
-    pl.semaphore_signal(barrier, inc=1, device_id={"seq": partner}, device_id_type=MESH)
+    def greet(k, carry):
+        pl.semaphore_signal(barrier, inc=1, device_id={"seq": (me + k) % n_seq}, device_id_type=MESH)
+        return carry
+
+    lax.fori_loop(1, n_seq, greet, 0)
     for b in bits:
         pl.semaphore_signal(barrier, inc=1, device_id={"head": flip(mine, b)}, device_id_type=MESH)
 
-    def greet(k, carry):
-        pl.semaphore_signal(barrier, inc=1, device_id={"seq": (me + 2 * k) % n_seq}, device_id_type=MESH)
-        return carry
-
-    lax.fori_loop(1, outer, greet, 0)
-    pl.semaphore_wait(barrier, outer + len(bits))
+    loads[0].wait()
+    row_at = lax.broadcasted_iota(jnp.int32, (entries, BLOCK), 0)
+    lane_at = lax.broadcasted_iota(jnp.int32, (BLOCK, entries), 1)
+
+    def count(h, carry):
+        total = jnp.zeros((1, entries), F32)
+        for b in range(nb):
+            code_row = codes_ref[pl.ds(h, 1), pl.ds(b * BLOCK, BLOCK)]
+            code_full = jnp.transpose(jnp.broadcast_to(code_row, (width, BLOCK)))
+            code_cols = jnp.concatenate([code_full] * (entries // width), axis=1)
+            one_f = (lane_at == code_cols).astype(F32)
+            hot[h, b] = one_f.astype(BF16)
+            counts = jnp.sum(one_f, axis=0, keepdims=True)
+            cnt_block[h, b] = counts
+            total += counts
+        cn_own[h] = total
+        return carry
+
+    lax.fori_loop(0, heads, count, 0)
+    pl.semaphore_wait(barrier, n_seq - 1 + len(bits))
 
     def gather_copy(src_mask, to, chunk):
         block = flip(mine, src_mask)
@@ -144,57 +162,26 @@
             src_ref=src, dst_ref=dst, send_sem=send, recv_sem=recv,
             device_id={"seq": to}, device_id_type=MESH)
 
-    count_pair = seq_copy(cn_own, cny_in, cny_s.at[0], cny_r.at[0], partner)
-
-    def count_chain(to):
-        return seq_copy(cnz_out, cnz_in, cnz_s.at[0], cnz_r.at[0], to)
-
-    loads[0].wait()
-    row_at = lax.broadcasted_iota(jnp.int32, (entries, BLOCK), 0)
-    lane_at = lax.broadcasted_iota(jnp.int32, (BLOCK, entries), 1)
-
-    def count(h, carry):
-        total = jnp.zeros((1, entries), F32)
+    def count_copy(to, source):
+        return seq_copy(cn_own, cn_in.at[source], cn_s.at[to], cn_r.at[source], to)
+
+    def send_counts(to, carry):
+        count_copy(to, me).start()
+        return carry
+
+    lax.fori_loop(me + 1, n_seq, send_counts, 0)
+
+    def take_counts():
+        def wait(source, carry):
+            count_copy(source, source).wait_recv()
+            return carry
+
+        lax.fori_loop(0, me, wait, 0)
+        before = lax.fori_loop(0, me, lambda j, total: total + cn_in[j], jnp.zeros(cn_own.shape, F32))
+        row = before
         for b in range(nb):
-            code_row = codes_ref[pl.ds(h, 1), pl.ds(b * BLOCK, BLOCK)]
-            code_full = jnp.transpose(jnp.broadcast_to(code_row, (width, BLOCK)))
-            code_cols = jnp.concatenate([code_full] * (entries // width), axis=1)
-            one_f = (lane_at == code_cols).astype(F32)
-            hot[h, b] = one_f.astype(BF16)
-            counts = jnp.sum(one_f, axis=0, keepdims=True)
-            cnt_block[h, b] = counts
-            total += counts
-        cn_own[h] = total
-        return carry
-
-    lax.fori_loop(0, heads, count, 0)
-    count_pair.start()
-
-    def share_counts():
-        count_pair.wait_recv()
-
-        @pl.when(jnp.logical_not(has_down))
-        def _():
-            cnz_in[...] = jnp.zeros(cnz_in.shape, F32)
-
-        @pl.when(has_down)
-        def _():
-            count_chain(me - 2).wait_recv()
-
-        cnz_out[...] = cnz_in[...] + cn_own[...] + cny_in[...]
-
-        @pl.when(has_up)
-        def _():
-            count_chain(me + 2).start()
-
-        def per_head(h, carry):
-            row = cnz_in[h] + cny_in[h] * is_hi
-            for b in range(nb):
-                cnt_pre[h, b] = row
-                row = row + cnt_block[h, b]
-            return carry
-
-        lax.fori_loop(0, heads, per_head, 0)
+            cnt_pre[:, b] = row
+            row = row + cnt_block[:, b]
 
     def prefix_pair(h):
         return seq_copy(py_out.at[h], py_in.at[h], py_s.at[h], py_r.at[h], partner)
@@ -210,30 +197,30 @@
 
     def sums(h, carry):
         head_lanes = pl.ds(pl.multiple_of(h * width, width), width)
-        book = cb_ref[h]
-        book_t[h] = jnp.transpose(book.astype(F32)).astype(BF16)
         for b in range(nb):
             rows = pl.ds(b * BLOCK, BLOCK)
-            code_row = codes_ref[pl.ds(h, 1), rows]
-            one_t = (row_at == code_row).astype(F32).astype(BF16)
+            one_t = (row_at == codes_ref[pl.ds(h, 1), rows]).astype(F32).astype(BF16)
             hot_t[h, b] = one_t
-            key = nn(hot[h, b], book)
-            keys[h, b] = key.astype(BF16)
-            keys_t[h, b] = jnp.transpose(key).astype(BF16)
             own[h, b] = nn(one_t, v_ref[rows, head_lanes])
         total = own[h, 0, other_half]
         for b in range(1, nb):
             total += own[h, b, other_half]
         py_out[h] = total.astype(BF16)
         prefix_pair(h).start()
-
-        @pl.when(h == jnp.minimum(at, heads - 1))
-        def _():
-            share_counts()
-
         return carry
 
     lax.fori_loop(0, heads, sums, 0)
+
+    def make_keys(h, carry):
+        book = cb_ref[h]
+        book_t[h] = jnp.transpose(book.astype(F32)).astype(BF16)
+        for b in range(nb):
+            key = nn(hot[h, b], book)
+            keys[h, b] = key.astype(BF16)
+            keys_t[h, b] = jnp.transpose(key).astype(BF16)
+        return carry
+
+    lax.fori_loop(0, heads, make_keys, 0)
 
     def prefix_chain(h):
         prefix_pair(h).wait_recv()
@@ -292,42 +279,55 @@
             cache_exp = jnp.exp2(cache_scores - highest)
             total = jnp.sum(local_exp, axis=0, keepdims=True) + jnp.sum(cache_exp * counts, axis=0, keepdims=True)
             inverse = 1.0 / total
-            lprob[h, b, seen * p // 2:seen * p // 2 + seen] = local_exp * inverse
-            cprob[h, b, p] = cache_exp * inverse
-
+            lanes = slice(p * TILE, seen)
+            local_low[h, b, 0:seen, lanes] = (local_exp * inverse).astype(BF16)
+            if seen < BLOCK:
+                local_low[h, b, seen:BLOCK, lanes] = jnp.zeros((BLOCK - seen, TILE), BF16)
+            cache_low[h, b, :, lanes] = (cache_exp * inverse).astype(BF16)
+
+    pairs = heads // 2
+    rounds = heads * nb // 2
+    turn = 2 * at
+
+    def chain_at(slot):
+        j = slot - turn
+
+        @pl.when((j >= 0) & (j < pairs))
+        def _():
+            prefix_chain(2 * j)
+            prefix_chain(2 * j + 1)
+
+    relay_at = {}
+    for chunk in range(chunks):
+        where = ("pre", "pre", 1, rounds - 1, "mid", rounds, rounds + 2, rounds + heads - 1)[8 * chunk // chunks]
+        relay_at.setdefault(where, []).append(chunk)
+
+    def relays(first, last, now):
+        for slot, which in relay_at.items():
+            if not isinstance(slot, str) and first <= slot < last:
+                @pl.when(now == slot - first)
+                def _(which=which):
+                    for chunk in which:
+                        relay(chunk)
+
+    def relay_named(name):
+        for chunk in relay_at.get(name, []):
+            relay(chunk)
+
+    chain_at(0)
+    take_counts()
+    chain_at(1)
+    relay_named("pre")
     loads[3].wait()
-    units = heads * nb
-    early = list(range(chunks // 2))
-    relay(early[0])
-    relay_at = {}
-    for j in early[1:]:
-        relay_at.setdefault(max(0, units * j // len(early) - 1), []).append(j)
-
-    def unit(u, carry):
-        h, b = u // nb, u % nb
-        softmax(h, b)
-
-        @pl.when(u < heads)
-        def _():
-            prefix_chain(u)
-
-        if units >= 2 * heads:
-            @pl.when((u >= heads) & (u < 2 * heads))
-            def _():
-                prefix_gather(u - heads)
-
-        for step, which in relay_at.items():
-            @pl.when(u == step)
-            def _(which=which):
-                for chunk in which:
-                    relay(chunk)
-
-        return carry
-
-    lax.fori_loop(0, units, unit, 0)
-    if units < 2 * heads:
-        for h in range(heads):
-            prefix_gather(h)
+
+    def unit(k, carry):
+        softmax(2 * k // nb, 2 * k % nb)
+        softmax((2 * k + 1) // nb, (2 * k + 1) % nb)
+        chain_at(k + 2)
+        relays(0, rounds, k)
+        return carry
+
+    lax.fori_loop(0, rounds, unit, 0)
     loads[4].wait()
 
     depth = go_in.shape[1]
@@ -339,46 +339,30 @@
             total += nt(gath[k, rows], w_ref[:, k * depth:(k + 1) * depth])
         dout[rows] = total.astype(BF16)
 
-    def value_pass(h, b, p):
+    def value_pass(h, b):
         head_lanes = pl.ds(pl.multiple_of(h * width, width), width)
-        grad = dout[pl.ds(b * BLOCK + p * TILE, TILE), head_lanes]
-        value = nn(cprob[h, b, p].astype(BF16), grad)
-        if p == 0:
-            vpart[h, b] = value
-        else:
-            vpart[h, b] += value
-
-    def grad_pass(h, b, p):
+        vpart[h, b] = nn(cache_low[h, b], dout[pl.ds(b * BLOCK, BLOCK), head_lanes])
+
+    def grad_pass(h, b):
         head_lanes = pl.ds(pl.multiple_of(h * width, width), width)
-        rows = pl.ds(b * BLOCK + p * TILE, TILE)
-        seen = (p + 1) * TILE
+        rows = pl.ds(b * BLOCK, BLOCK)
         query = q_ref[rows, head_lanes]
         grad = dout[rows, head_lanes]
-        counts = jnp.concatenate([cnt_full[h, b]] * (TILE // width), axis=1)
-        local_grad = nt(v_ref[pl.ds(b * BLOCK, seen), head_lanes], grad)
+        counts = jnp.concatenate([cnt_full[h, b]] * (BLOCK // width), axis=1)
+        local_grad = nt(v_ref[rows, head_lanes], grad)
         cache_grad = nt(cval[h, b], grad)
-        local_prob = lprob[h, b, seen * p // 2:seen * p // 2 + seen]
-        cache_prob = cprob[h, b, p]
-        local_low = local_prob.astype(BF16)
-        cache_low = cache_prob.astype(BF16)
-        delta = (jnp.sum(local_low.astype(F32) * local_grad, axis=0, keepdims=True)
-                 + jnp.sum(cache_low.astype(F32) * cache_grad, axis=0, keepdims=True))
+        local_prob = local_low[h, b].astype(F32)
+        cache_prob = cache_low[h, b].astype(F32)
+        delta = (jnp.sum(local_prob * local_grad, axis=0, keepdims=True)
+                 + jnp.sum(cache_prob * cache_grad, axis=0, keepdims=True))
         local_score_grad = (local_prob * (local_grad - delta) * scale).astype(BF16)
         cache_score_grad = (cache_prob * (cache_grad - delta * counts) * scale).astype(BF16)
-        gq_t = nn(keys_t[h, b, :, 0:seen], local_score_grad) + nn(book_t[h], cache_score_grad)
+        gq_t = nn(keys_t[h, b], local_score_grad) + nn(book_t[h], cache_score_grad)
         gq_ref[rows, head_lanes] = jnp.transpose(gq_t).astype(BF16)
-        code = nn(cache_score_grad, query)
-        key_grad = nn(local_score_grad, query)
-        local = nn(local_low, grad)
-        last = p * TILE
-        if p > 0:
-            key_acc[h, 0:last] += key_grad[0:last]
-            local_part[h, b, 0:last] += local[0:last]
-        key_acc[h, last:seen] = key_grad[last:seen]
-        local_part[h, b, last:seen] = local[last:seen]
-        if p == parts - 1:
-            code += nn(hot_t[h, b], key_acc[h].astype(BF16))
-        if b == 0 and p == 0:
+        key_grad = nn(local_score_grad, query).astype(BF16)
+        code = nn(hot_t[h, b], key_grad) + nn(cache_score_grad, query)
+        local_part[h, b] = nn(local_low[h, b], grad)
+        if b == 0:
             code_acc[h] = code
         else:
             code_acc[h] += code
@@ -486,42 +470,41 @@
         code_half(h, 1 - side).wait_recv()
         gc_ref[h, other_half] = c_fin[h, 1 - side].astype(F32).reshape(half, width)
 
-    tiles = nb * parts
-    slots = max(1, (tiles - 1) * heads)
-    late = list(range(chunks // 2, chunks))
-    late_at = {}
-    for j, chunk in enumerate(late):
-        late_at.setdefault(min(slots - 1, slots * j // len(late) + 1), []).append(chunk)
-
-    for g in range(tiles):
-        b, p = g // parts, g % parts
-        final = g == tiles - 1
-        if final:
-            for chunk in late:
-                for m, _ in plan:
-                    if m != 0 and (m, chunk) not in taken:
-                        relay(chunk)
-        for chunk in range(g * per_tile, (g + 1) * per_tile):
-            for slot in by_slot:
-                arrive(slot, chunk)
-        project(g * TILE)
-
-        def values(h, carry, b=b, p=p, final=final):
-            value_pass(h, b, p)
+    for b in range(nb):
+        final = b == nb - 1
+        for part in range(parts):
+            start = b * BLOCK + part * TILE
+            for chunk in range(start // CHUNK, (start + TILE) // CHUNK):
+                for slot in by_slot:
+                    arrive(slot, chunk)
+            project(start)
+        if b == 0:
+            relay_named("mid")
+
+            def rest(j, carry):
+                @pl.when(turn + j >= rounds + 2)
+                def _():
+                    prefix_chain(2 * j)
+                    prefix_chain(2 * j + 1)
+
+                return carry
+
+            lax.fori_loop(0, pairs, rest, 0)
+
+        def values(h, carry, b=b, final=final):
+            value_pass(h, b)
             if final:
                 send_later(h)
             return carry
 
         lax.fori_loop(0, heads, values, 0)
 
-        def grads(h, carry, g=g, b=b, p=p, final=final):
-            grad_pass(h, b, p)
-            for slot, which in late_at.items():
-                if slot // heads == g:
-                    @pl.when(h == slot % heads)
-                    def _(which=which):
-                        for chunk in which:
-                            relay(chunk)
+        def grads(h, carry, b=b, final=final):
+            if b == 0:
+                prefix_gather(h)
+            grad_pass(h, b)
+            if b == 0:
+                relays(rounds, rounds + heads, h)
             if final:
                 send_code(h)
 
@@ -537,28 +520,36 @@
     soon = behind * 2 < outer
     last_ones = behind * 4 >= 3 * outer
 
+    @pl.when(behind == 0)
+    def _():
+        later_chain(heads - 1)
+
+    def chain_step(h, carry):
+        @pl.when(soon & (behind > 0))
+        def _():
+            later_chain(h)
+
+        return carry
+
+    lax.fori_loop(0, heads, chain_step, 0)
+
     def reduce_step(h, carry):
-        @pl.when(soon & (has_up | (h == heads - 1)))
+        reduce_code(h)
+
+        @pl.when(jnp.logical_not(soon | last_ones))
         def _():
             later_chain(h)
 
-        reduce_code(h)
-
-        @pl.when(jnp.logical_not(soon | last_ones))
+        return carry
+
+    lax.fori_loop(0, heads, reduce_step, 0)
+
+    def spread_step(h, carry):
+        @pl.when(last_ones)
         def _():
             later_chain(h)
 
-        return carry
-
-    lax.fori_loop(0, heads, reduce_step, 0)
-
-    def spread_step(h, carry):
         spread_code(h)
-
-        @pl.when(last_ones)
-        def _():
-            later_chain(h)
-
         return carry
 
     lax.fori_loop(0, heads, spread_step, 0)
@@ -597,15 +588,24 @@
         return carry
 
     lax.fori_loop(0, heads, drain, 0)
-    count_pair.wait_send()
-
-    @pl.when(has_up)
-    def _():
-        count_chain(me + 2).wait_send()
-
+
+    def drain_counts(to, carry):
+        count_copy(to, me).wait_send()
+        return carry
+
+    lax.fori_loop(me + 1, n_seq, drain_counts, 0)
     for m, b in plan:
         for chunk in range(chunks):
             gather_copy(m, b, chunk).wait_send()
+
+
+def write_out(*refs):
+    sems = refs[-1]
+    copies = [pltpu.make_async_copy(refs[k], refs[k + 3], sems.at[k]) for k in range(3)]
+    for copy in copies:
+        copy.start()
+    for copy in copies:
+        copy.wait()
 
 
 def per_device(queries, values, codes, codebook, out_weight, grad_out):
@@ -622,7 +622,7 @@
     halves = pltpu.VMEM((heads, half, width), BF16)
     pieces = pltpu.VMEM((heads, n_seq // 2, entries // n_seq, width), BF16)
     counts = pltpu.VMEM((heads, 1, entries), F32)
-    return pl.pallas_call(
+    results = pl.pallas_call(
         functools.partial(kernel, n_seq, n_head),
         out_shape=(
             jax.ShapeDtypeStruct(queries.shape, BF16),
@@ -649,25 +649,32 @@
             pltpu.VMEM((heads, nb, 1, entries), F32),
             pltpu.VMEM((heads, nb, entries, width), F32),
             pltpu.VMEM((heads, nb, entries, width), BF16),
-            pltpu.VMEM((heads, nb, (parts + 1) * BLOCK // 2, TILE), F32),
-            pltpu.VMEM((heads, nb, parts, entries, TILE), F32),
-            pltpu.VMEM((heads, BLOCK, width), F32),
+            pltpu.VMEM((heads, nb, BLOCK, BLOCK), BF16),
+            pltpu.VMEM((heads, nb, entries, BLOCK), BF16),
             pltpu.VMEM((heads, nb, BLOCK, width), F32),
             pltpu.VMEM((heads, nb, entries, width), F32),
             pltpu.VMEM((heads, entries, width), F32),
             pltpu.VMEM((heads, entries, width), F32),
-            counts, counts, counts, counts,
+            counts, pltpu.VMEM((n_seq, heads, 1, entries), F32),
             halves, halves, halves, halves, halves, halves,
             halves, halves, halves, halves, halves, halves,
             halves, halves, pieces, pieces,
             pltpu.VMEM((heads, 2, n_seq // 2, entries // n_seq, width), BF16),
             dma((5,)), dma((chunks,)),
             dma((n_head, chunks)), dma((n_head, chunks)),
-            dma((1,)), dma((1,)), dma((1,)), dma((1,)),
+            dma((n_seq,)), dma((n_seq,)),
         ] + [dma((heads,))] * 16 + [dma((heads, n_seq // 2))] * 4,
         compiler_params=pltpu.CompilerParams(
-            collective_id=0, has_side_effects=True, vmem_limit_bytes=57 * 1024 * 1024),
-    )(queries, values, codes.T, codebook, out_weight, grad_out)
+            collective_id=0, has_side_effects=True, vmem_limit_bytes=50 * 1024 * 1024),
+    )(*(pltpu.with_memory_space_constraint(x, pltpu.HBM) for x in (queries, values, codes.T, codebook, out_weight, grad_out)))
+    return pl.pallas_call(
+        write_out,
+        out_shape=tuple(jax.ShapeDtypeStruct(r.shape, r.dtype) for r in results),
+        in_specs=[vmem] * 3,
+        out_specs=(hbm,) * 3,
+        scratch_shapes=[dma((3,))],
+        compiler_params=pltpu.CompilerParams(vmem_limit_bytes=1024 * 1024),
+    )(*results)
 
 
 def solution(mesh):

time: 91 us -> 74.1 us (0.81)
  Pallas kernels: 85.8 us -> 73.2 us
  local copies, waits for them, and re-layouts: 4.36 us -> 0 us
    pallas_call x1, Pallas kernels: 85.8 us -> 71.5 us  [per_device(): pl.pallas_call(functools.partial(kernel, n_seq, n_head), out_shape=(jax.S...]
    unnamed x7 -> x0, local copies, waits for them, and re-layouts: 4.36 us -> none
    pallas_call x0 -> x1, Pallas kernels: none -> 1.69 us  [per_device(): pl.pallas_call(write_out, out_shape=tuple((jax.ShapeDtypeStruct(r.shape,...]
where the time goes in v2:
time: 74.1 us; the launch traced here: 73.8 us
  Pallas kernels  73.2 us (99%)
    pallas_call x1, Pallas kernels, per_device(): pl.pallas_call(functools.partial(kernel, n_seq, n_head), out_shape=(jax.S...  71.5 us
    pallas_call x1, Pallas kernels, per_device(): pl.pallas_call(write_out, out_shape=tuple((jax.ShapeDtypeStruct(r.shape,...  1.69 us

profile of v2, /device:TPU:0, one launch (start us, length us, event | category | flops | bytes accessed | tf_op | source)
XLA Modules:
  0.0 73.8 jit_solution(6182673940204079526)
XLA Ops:
  0.6 71.5 %shard_map.85 = (bf16[1024,512]{1,0:T(8,128)(2,1)S(1)}, bf16[1024,512]{1,0:T(8,128)(2,1)S(1)}, f32[4,512,128]{2,1,0:T(8,128)S(1)}) custom-call(bf16[1024,512]{1,0:T(8,128)(2,1)} %q_in.1, bf16[1024,512]{1,0:T(8,128)(2,1)} %v_in.1, s32[4,1024]{1,0:T(4,128)} %bitcast.1, bf16[4,512,128]{2,1,0:T(8,128)(2,1)} %cb_in.1, bf16[512,2048]{1,0:T(8,128)(2,1)} %w_in.1, ...), custom_call_target="tpu_custom_call" | custom-call | tf_op jit(solution)/shard_map/pallas_call | solution.py:625
  72.2 1.7 %shard_map.86 = (bf16[1024,512]{1,0:T(8,128)(2,1)}, bf16[1024,512]{1,0:T(8,128)(2,1)}, f32[4,512,128]{2,1,0:T(8,128)}) custom-call(bf16[1024,512]{1,0:T(8,128)(2,1)S(1)} %get-tuple-element.6.refs_0_, bf16[1024,512]{1,0:T(8,128)(2,1)S(1)} %get-tuple-element.7.refs_1_, f32[4,512,128]{2,1,0:T(8,128)S(1)} %get-tuple-element.8.refs_2_), custom_call_target="tpu_custom_call" | custom-call | tf_op jit(solution)/shard_map/pallas_call | solution.py:670

commit v3 on v2

--- a/solution.py
+++ b/solution.py
@@ -10,6 +10,7 @@
 BLOCK = 512
 TILE = 256
 CHUNK = 128
+SUBS = 2
 NEG = -1e30
 LOG2E = 1.4426950408889634
 F32 = jnp.float32
@@ -35,11 +36,11 @@
     cn_own, cn_in,
     py_out, py_in, pz_out, pz_in, pa_out, pa_in,
     ly_out, ly_in, lz_out, lz_in, la_out, la_in,
-    cy_out, cy_in, cz_out, cz_in, c_fin,
+    cy_out, cy_in, c_out, c_below, c_above, c_fin,
     load_s, go_s, ag_s, ag_r, cn_s, cn_r,
     py_s, py_r, pz_s, pz_r, pa_s, pa_r,
     ly_s, ly_r, lz_s, lz_r, la_s, la_r,
-    cy_s, cy_r, ca_s, ca_r, cz_s, cz_r, cf_s, cf_r,
+    cy_s, cy_r, c_s, cb_r, cu_r, cp_s, cp_r, fu_s, fd_s, cf_r,
 ):
     rows_all = q_ref.shape[0]
     heads, entries, width = cb_ref.shape
@@ -49,7 +50,8 @@
     per_tile = TILE // CHUNK
     outer = n_seq // 2
     half = entries // 2
-    piece = half // outer
+    piece = half // SUBS
+    center = outer // 2
     scale = width ** (-0.5)
     me = lax.axis_index("seq")
     mine = lax.axis_index("head")
@@ -285,21 +287,19 @@
                 local_low[h, b, seen:BLOCK, lanes] = jnp.zeros((BLOCK - seen, TILE), BF16)
             cache_low[h, b, :, lanes] = (cache_exp * inverse).astype(BF16)
 
-    pairs = heads // 2
     rounds = heads * nb // 2
     turn = 2 * at
 
     def chain_at(slot):
-        j = slot - turn
-
-        @pl.when((j >= 0) & (j < pairs))
-        def _():
-            prefix_chain(2 * j)
-            prefix_chain(2 * j + 1)
+        h = slot - turn
+
+        @pl.when((h >= 0) & (h < heads))
+        def _():
+            prefix_chain(h)
 
     relay_at = {}
     for chunk in range(chunks):
-        where = ("pre", "pre", 1, rounds - 1, "mid", rounds, rounds + 2, rounds + heads - 1)[8 * chunk // chunks]
+        where = (0, 1, rounds - 1, "mid", "late", rounds, rounds + 2, rounds + heads - 1)[8 * chunk // chunks]
         relay_at.setdefault(where, []).append(chunk)
 
     def relays(first, last, now):
@@ -317,7 +317,6 @@
     chain_at(0)
     take_counts()
     chain_at(1)
-    relay_named("pre")
     loads[3].wait()
 
     def unit(k, carry):
@@ -407,7 +406,6 @@
             later_hop(h, me - 2).start()
 
         la_out[h] = (above + total * is_hi).astype(BF16)
-        later_back(h).start()
         later_ref[h, own_half] = above + pair * is_lo
 
     def later_gather(h):
@@ -424,51 +422,79 @@
     def code_pair(h):
         return seq_copy(cy_out.at[h], cy_in.at[h], cy_s.at[h], cy_r.at[h], partner)
 
-    def code_out(h, to, source):
-        return seq_copy(
-            cz_out.at[h, to], cz_in.at[h, source], cz_s.at[h, to], cz_r.at[h, source], 2 * to + side)
-
-    def code_back(h, to, source):
-        return seq_copy(
-            c_fin.at[h, side, source], c_fin.at[h, side, source], cf_s.at[h, to], cf_r.at[h, source], 2 * to + side)
-
-    def code_half(h, which):
-        return seq_copy(c_fin.at[h, which], c_fin.at[h, which], ca_s.at[h], ca_r.at[h], partner)
-
-    def over_chain(action):
-        def body(k, carry):
-            action((at + k) % outer)
-            return carry
-
-        lax.fori_loop(1, outer, body, 0)
+    def code_up(h, s):
+        return seq_copy(c_out.at[h, s], c_below.at[h, s], c_s.at[h, s], cb_r.at[h, s], me + 2)
+
+    def code_down(h, s):
+        return seq_copy(c_out.at[h, s], c_above.at[h, s], c_s.at[h, s], cu_r.at[h, s], me - 2)
+
+    def fin_up(h, s):
+        return seq_copy(c_fin.at[h, side, s], c_fin.at[h, side, s], fu_s.at[h, s], cf_r.at[h, s], me + 2)
+
+    def fin_down(h, s):
+        return seq_copy(c_fin.at[h, side, s], c_fin.at[h, side, s], fd_s.at[h, s], cf_r.at[h, s], me - 2)
+
+    def fin_pair(h, which, s):
+        return seq_copy(c_fin.at[h, which, s], c_fin.at[h, which, s], cp_s.at[h, s], cp_r.at[h, s], partner)
 
     def send_code(h):
         cy_out[h] = code_acc[h, other_half].astype(BF16)
         code_pair(h).start()
 
+    def piece_of(which, s):
+        return pl.ds(pl.multiple_of(which * half + s * piece, piece), piece)
+
     def reduce_code(h):
         code_pair(h).wait_recv()
-        total = code_acc[h, own_half] + cy_in[h].astype(F32)
-        cz_out[h] = total.astype(BF16).reshape(outer, piece, width)
-        over_chain(lambda to: code_out(h, to, at).start())
-        cz_in[h, at] = cz_out[h, at]
+        code_acc[h, own_half] += cy_in[h].astype(F32)
+        for s in range(SUBS):
+            span = piece_of(side, s)
+
+            @pl.when((at <= center) & has_down)
+            def _(s=s, span=span):
+                code_up(h, s).wait_recv()
+                code_acc[h, span] += c_below[h, s].astype(F32)
+
+            @pl.when((at >= center) & has_up)
+            def _(s=s, span=span):
+                code_down(h, s).wait_recv()
+                code_acc[h, span] += c_above[h, s].astype(F32)
+
+            c_out[h, s] = code_acc[h, span].astype(BF16)
+
+            @pl.when(at < center)
+            def _(s=s):
+                code_up(h, s).start()
+
+            @pl.when(at > center)
+            def _(s=s):
+                code_down(h, s).start()
 
     def spread_code(h):
-        over_chain(lambda source: code_out(h, source, source).wait_recv())
-        total = cz_in[h, 0].astype(F32)
-        for k in range(1, outer):
-            total += cz_in[h, k].astype(F32)
-        c_fin[h, side, at] = total.astype(BF16)
-        over_chain(lambda to: code_back(h, to, at).start())
-
-    def pair_code(h):
-        over_chain(lambda source: code_back(h, source, source).wait_recv())
-        code_half(h, side).start()
-        gc_ref[h, own_half] = c_fin[h, side].astype(F32).reshape(half, width)
+        for s in range(SUBS):
+            @pl.when(at == center)
+            def _(s=s):
+                c_fin[h, side, s] = c_out[h, s]
+
+            @pl.when(at != center)
+            def _(s=s):
+                fin_up(h, s).wait_recv()
+
+            @pl.when((at <= center) & has_down)
+            def _(s=s):
+                fin_down(h, s).start()
+
+            @pl.when((at >= center) & has_up)
+            def _(s=s):
+                fin_up(h, s).start()
+
+            fin_pair(h, side, s).start()
+            gc_ref[h, piece_of(side, s)] = c_fin[h, side, s].astype(F32)
 
     def last_code(h):
-        code_half(h, 1 - side).wait_recv()
-        gc_ref[h, other_half] = c_fin[h, 1 - side].astype(F32).reshape(half, width)
+        for s in range(SUBS):
+            fin_pair(h, 1 - side, s).wait_recv()
+            gc_ref[h, piece_of(1 - side, s)] = c_fin[h, 1 - side, s].astype(F32)
 
     for b in range(nb):
         final = b == nb - 1
@@ -478,19 +504,10 @@
                 for slot in by_slot:
                     arrive(slot, chunk)
             project(start)
-        if b == 0:
-            relay_named("mid")
-
-            def rest(j, carry):
-                @pl.when(turn + j >= rounds + 2)
-                def _():
-                    prefix_chain(2 * j)
-                    prefix_chain(2 * j + 1)
-
-                return carry
-
-            lax.fori_loop(0, pairs, rest, 0)
-
+            if b == 0:
+                if part == 0:
+                    relay_named("mid")
+                chain_at(rounds + 2 + part)
         def values(h, carry, b=b, final=final):
             value_pass(h, b)
             if final:
@@ -498,6 +515,17 @@
             return carry
 
         lax.fori_loop(0, heads, values, 0)
+        if b == 0:
+            relay_named("late")
+
+            def rest(h, carry):
+                @pl.when(turn + h >= rounds + 2 + parts)
+                def _():
+                    prefix_chain(h)
+
+                return carry
+
+            lax.fori_loop(0, heads, rest, 0)
 
         def grads(h, carry, b=b, final=final):
             if b == 0:
@@ -518,7 +546,6 @@
 
     behind = outer - 1 - at
     soon = behind * 2 < outer
-    last_ones = behind * 4 >= 3 * outer
 
     @pl.when(behind == 0)
     def _():
@@ -536,67 +563,101 @@
     def reduce_step(h, carry):
         reduce_code(h)
 
-        @pl.when(jnp.logical_not(soon | last_ones))
+        @pl.when(at == center)
+        def _():
+            spread_code(h)
+
+        @pl.when(jnp.logical_not(soon) & has_down)
         def _():
             later_chain(h)
+            later_back(h).start()
 
         return carry
 
     lax.fori_loop(0, heads, reduce_step, 0)
 
-    def spread_step(h, carry):
-        @pl.when(last_ones)
+    def back_step(h, carry):
+        @pl.when(jnp.logical_not(soon | has_down))
         def _():
             later_chain(h)
 
-        spread_code(h)
-        return carry
-
-    lax.fori_loop(0, heads, spread_step, 0)
-
-    def pair_step(h, carry):
-        pair_code(h)
-        later_gather(h)
-        return carry
-
-    lax.fori_loop(0, heads, pair_step, 0)
-
-    def last_step(h, carry):
-        last_code(h)
-        return carry
-
-    lax.fori_loop(0, heads, last_step, 0)
-
-    def drain(h, carry):
+        @pl.when(soon | jnp.logical_not(has_down))
+        def _():
+            later_back(h).start()
+
+        return carry
+
+    lax.fori_loop(0, heads, back_step, 0)
+
+    def drain_early(h, carry):
         prefix_pair(h).wait_send()
         prefix_back(h).wait_send()
-        later_pair(h).wait_send()
-        later_back(h).wait_send()
 
         @pl.when(has_up)
         def _():
             prefix_hop(h, me + 2).wait_send()
 
-        @pl.when(has_down)
-        def _():
-            later_hop(h, me - 2).wait_send()
-
-        code_pair(h).wait_send()
-        code_half(h, side).wait_send()
-        over_chain(lambda to: code_out(h, to, at).wait_send())
-        over_chain(lambda to: code_back(h, to, at).wait_send())
-        return carry
-
-    lax.fori_loop(0, heads, drain, 0)
+        return carry
+
+    lax.fori_loop(0, heads, drain_early, 0)
 
     def drain_counts(to, carry):
         count_copy(to, me).wait_send()
         return carry
 
     lax.fori_loop(me + 1, n_seq, drain_counts, 0)
+
     for m, b in plan:
         for chunk in range(chunks):
             gather_copy(m, b, chunk).wait_send()
+
+    def spread_step(h, carry):
+        @pl.when(at != center)
+        def _():
+            spread_code(h)
+
+        return carry
+
+    lax.fori_loop(0, heads, spread_step, 0)
+
+    def last_step(h, carry):
+        later_gather(h)
+        last_code(h)
+        return carry
+
+    lax.fori_loop(0, heads, last_step, 0)
+
+    def drain(h, carry):
+        later_pair(h).wait_send()
+        later_back(h).wait_send()
+
+        @pl.when(has_down)
+        def _():
+            later_hop(h, me - 2).wait_send()
+
+        code_pair(h).wait_send()
+        for s in range(SUBS):
+            @pl.when(at < center)
+            def _(s=s):
+                code_up(h, s).wait_send()
+
+            @pl.when(at > center)
+            def _(s=s):
+                code_down(h, s).wait_send()
+
+            @pl.when((at <= center) & has_down)
+            def _(s=s):
+                fin_down(h, s).wait_send()
+
+            @pl.when((at >= center) & has_up)
+            def _(s=s):
+                fin_up(h, s).wait_send()
+
+            fin_pair(h, side, s).wait_send()
+
+        return carry
+
+    lax.fori_loop(0, heads, drain, 0)
 
 
 def write_out(*refs):
@@ -620,7 +681,7 @@
     vmem = pl.BlockSpec(memory_space=pltpu.VMEM)
     dma = pltpu.SemaphoreType.DMA
     halves = pltpu.VMEM((heads, half, width), BF16)
-    pieces = pltpu.VMEM((heads, n_seq // 2, entries // n_seq, width), BF16)
+    pieces = pltpu.VMEM((heads, SUBS, half // SUBS, width), BF16)
     counts = pltpu.VMEM((heads, 1, entries), F32)
     results = pl.pallas_call(
         functools.partial(kernel, n_seq, n_head),
@@ -658,12 +719,12 @@
             counts, pltpu.VMEM((n_seq, heads, 1, entries), F32),
             halves, halves, halves, halves, halves, halves,
             halves, halves, halves, halves, halves, halves,
-            halves, halves, pieces, pieces,
-            pltpu.VMEM((heads, 2, n_seq // 2, entries // n_seq, width), BF16),
+            halves, halves, pieces, pieces, pieces,
+            pltpu.VMEM((heads, 2, SUBS, half // SUBS, width), BF16),
             dma((5,)), dma((chunks,)),
             dma((n_head, chunks)), dma((n_head, chunks)),
             dma((n_seq,)), dma((n_seq,)),
-        ] + [dma((heads,))] * 16 + [dma((heads, n_seq // 2))] * 4,
+        ] + [dma((heads,))] * 14 + [dma((heads, SUBS))] * 8,
         compiler_params=pltpu.CompilerParams(
             collective_id=0, has_side_effects=True, vmem_limit_bytes=50 * 1024 * 1024),
     )(*(pltpu.with_memory_space_constraint(x, pltpu.HBM) for x in (queries, values, codes.T, codebook, out_weight, grad_out)))

time: 74.1 us -> 67.2 us (0.907)
  Pallas kernels: 73.2 us -> 66.3 us
    pallas_call x1, Pallas kernels: 71.5 us -> 64.6 us  [per_device(): pl.pallas_call(functools.partial(kernel, n_seq, n_head), out_shape=(jax.S...]
where the time goes in v3:
time: 67.2 us; the launch traced here: 67 us
  Pallas kernels  66.3 us (99%)
    pallas_call x1, Pallas kernels, per_device(): pl.pallas_call(functools.partial(kernel, n_seq, n_head), out_shape=(jax.S...  64.6 us
    pallas_call x1, Pallas kernels, per_device(): pl.pallas_call(write_out, out_shape=tuple((jax.ShapeDtypeStruct(r.shape,...  1.69 us

profile of v3, /device:TPU:0, one launch (start us, length us, event | category | flops | bytes accessed | tf_op | source)
XLA Modules:
  0.0 67.0 jit_solution(2604673832271393846)
XLA Ops:
  0.6 64.6 %shard_map.85 = (bf16[1024,512]{1,0:T(8,128)(2,1)S(1)}, bf16[1024,512]{1,0:T(8,128)(2,1)S(1)}, f32[4,512,128]{2,1,0:T(8,128)S(1)}) custom-call(bf16[1024,512]{1,0:T(8,128)(2,1)} %q_in.1, bf16[1024,512]{1,0:T(8,128)(2,1)} %v_in.1, s32[4,1024]{1,0:T(4,128)} %bitcast.1, bf16[4,512,128]{2,1,0:T(8,128)(2,1)} %cb_in.1, bf16[512,2048]{1,0:T(8,128)(2,1)} %w_in.1, ...), custom_call_target="tpu_custom_call" | custom-call | tf_op jit(solution)/shard_map/pallas_call | solution.py:686
  65.3 1.7 %shard_map.86 = (bf16[1024,512]{1,0:T(8,128)(2,1)}, bf16[1024,512]{1,0:T(8,128)(2,1)}, f32[4,512,128]{2,1,0:T(8,128)}) custom-call(bf16[1024,512]{1,0:T(8,128)(2,1)S(1)} %get-tuple-element.6.refs_0_, bf16[1024,512]{1,0:T(8,128)(2,1)S(1)} %get-tuple-element.7.refs_1_, f32[4,512,128]{2,1,0:T(8,128)S(1)} %get-tuple-element.8.refs_2_), custom_call_target="tpu_custom_call" | custom-call | tf_op jit(solution)/shard_map/pallas_call | solution.py:731

commit v4 on v3

--- a/solution.py
+++ b/solution.py
@@ -33,11 +33,11 @@
     q_ref, v_ref, codes_ref, cb_ref, w_ref, gath, dout,
     hot_t, hot, keys, keys_t, book_t, own, cnt_block, cnt_pre, cnt_full, cval,
     local_low, cache_low, local_part, vpart, code_acc, later_ref,
-    cn_own, cn_in,
+    cn_own, cny_in, cnz_out, cnz_in,
     py_out, py_in, pz_out, pz_in, pa_out, pa_in,
     ly_out, ly_in, lz_out, lz_in, la_out, la_in,
     cy_out, cy_in, c_out, c_below, c_above, c_fin,
-    load_s, go_s, ag_s, ag_r, cn_s, cn_r,
+    load_s, go_s, ag_s, ag_r, ax_r, cny_s, cny_r, cnz_s, cnz_r,
     py_s, py_r, pz_s, pz_r, pa_s, pa_r,
     ly_s, ly_r, lz_s, lz_r, la_s, la_r,
     cy_s, cy_r, c_s, cb_r, cu_r, cp_s, cp_r, fu_s, fd_s, cf_r,
@@ -76,9 +76,9 @@
                 index = index + b - 2 * b * ((index // b) % 2)
         return index
 
-    def go_load(chunk):
-        span = pl.ds(chunk * CHUNK, CHUNK)
-        return pltpu.make_async_copy(go_in.at[span], gath.at[mine, span], go_s.at[chunk])
+    def go_load(first, last):
+        span = pl.ds(first * CHUNK, (last - first) * CHUNK)
+        return pltpu.make_async_copy(go_in.at[span], gath.at[mine, span], go_s.at[min(first, 1)])
 
     loads = [
         pltpu.make_async_copy(src, dst, load_s.at[k])
@@ -86,17 +86,22 @@
             ((codes_in, codes_ref), (cb_in, cb_ref), (v_in, v_ref), (q_in, q_ref), (w_in, w_ref)))
     ]
     loads[0].start()
-    for chunk in range(chunks):
-        go_load(chunk).start()
+    go_load(0, 1).start()
+    go_load(1, chunks).start()
     for copy in loads[1:]:
         copy.start()
 
     barrier = pltpu.get_barrier_semaphore()
-    def greet(k, carry):
-        pl.semaphore_signal(barrier, inc=1, device_id={"seq": (me + k) % n_seq}, device_id_type=MESH)
-        return carry
-
-    lax.fori_loop(1, n_seq, greet, 0)
+    pl.semaphore_signal(barrier, inc=1, device_id={"seq": partner}, device_id_type=MESH)
+
+    @pl.when(has_down)
+    def _():
+        pl.semaphore_signal(barrier, inc=1, device_id={"seq": me - 2}, device_id_type=MESH)
+
+    @pl.when(has_up)
+    def _():
+        pl.semaphore_signal(barrier, inc=1, device_id={"seq": me + 2}, device_id_type=MESH)
+
     for b in bits:
         pl.semaphore_signal(barrier, inc=1, device_id={"head": flip(mine, b)}, device_id_type=MESH)
 
@@ -119,7 +124,8 @@
         return carry
 
     lax.fori_loop(0, heads, count, 0)
-    pl.semaphore_wait(barrier, n_seq - 1 + len(bits))
+    pl.semaphore_wait(
+        barrier, 1 + len(bits) + jnp.where(has_down, 1, 0) + jnp.where(has_up, 1, 0))
 
     def gather_copy(src_mask, to, chunk):
         block = flip(mine, src_mask)
@@ -127,7 +133,7 @@
         slot = src_mask ^ to
         return pltpu.make_async_remote_copy(
             src_ref=gath.at[block, span], dst_ref=gath.at[block, span],
-            send_sem=ag_s.at[slot, chunk], recv_sem=ag_r.at[slot, chunk],
+            send_sem=ag_s.at[0], recv_sem=ax_r.at[rank[slot], chunk] if slot in feeds else ag_r.at[rank[slot], chunk // per_tile],
             device_id={"head": flip(mine, to)}, device_id_type=MESH)
 
     plan = []
@@ -136,8 +142,14 @@
         plan += [(m, b) for m in known]
         known += [m ^ b for m in known]
     by_slot = {m ^ b: (m, b) for m, b in plan}
+    feeds = {m for m, _ in plan if m != 0}
+    rank = {slot: k for k, slot in enumerate(sorted(feeds))}
+    rank.update({slot: k for k, slot in enumerate(sorted(set(by_slot) - feeds))})
     for chunk in range(chunks):
-        go_load(chunk).wait()
+        if chunk == 0:
+            go_load(0, 1).wait()
+        elif chunk == 1:
+            go_load(1, chunks).wait()
         for m, b in plan:
             if m == 0 and b == bits[0]:
                 gather_copy(m, b, chunk).start()
@@ -147,6 +159,21 @@
                 gather_copy(m, b, chunk).start()
     taken = set()
 
+    def tile_copy(slot, start):
+        m, b = by_slot[slot]
+        block = flip(mine, m)
+        span = pl.ds(start, TILE)
+        return pltpu.make_async_remote_copy(
+            src_ref=gath.at[block, span], dst_ref=gath.at[block, span],
+            send_sem=ag_s.at[0], recv_sem=ag_r.at[rank[slot], start // TILE],
+            device_id={"head": flip(mine, b)}, device_id_type=MESH)
+
+    def all_sent():
+        span = gath.at[pl.ds(0, len(plan))]
+        return pltpu.make_async_remote_copy(
+            src_ref=span, dst_ref=span, send_sem=ag_s.at[0], recv_sem=ag_r.at[0, 0],
+            device_id={"head": flip(mine, bits[0])}, device_id_type=MESH)
+
     def arrive(slot, chunk):
         if (slot, chunk) not in taken:
             taken.add((slot, chunk))
@@ -164,35 +191,42 @@
             src_ref=src, dst_ref=dst, send_sem=send, recv_sem=recv,
             device_id={"seq": to}, device_id_type=MESH)
 
-    def count_copy(to, source):
-        return seq_copy(cn_own, cn_in.at[source], cn_s.at[to], cn_r.at[source], to)
-
-    def send_counts(to, carry):
-        count_copy(to, me).start()
-        return carry
-
-    lax.fori_loop(me + 1, n_seq, send_counts, 0)
+    count_pair = seq_copy(cn_own, cny_in, cny_s.at[0], cny_r.at[0], partner)
+    count_pair.start()
+
+    def count_hop(to):
+        return seq_copy(cnz_out, cnz_in, cnz_s.at[0], cnz_r.at[0], to)
 
     def take_counts():
-        def wait(source, carry):
-            count_copy(source, source).wait_recv()
-            return carry
-
-        lax.fori_loop(0, me, wait, 0)
-        before = lax.fori_loop(0, me, lambda j, total: total + cn_in[j], jnp.zeros(cn_own.shape, F32))
-        row = before
+        count_pair.wait_recv()
+
+        @pl.when(jnp.logical_not(has_down))
+        def _():
+            cnz_in[...] = jnp.zeros(cnz_in.shape, F32)
+
+        @pl.when(has_down)
+        def _():
+            count_hop(me - 2).wait_recv()
+
+        cnz_out[...] = cnz_in[...] + cn_own[...] + cny_in[...]
+
+        @pl.when(has_up)
+        def _():
+            count_hop(me + 2).start()
+
+        row = cnz_in[...] + cny_in[...] * is_hi
         for b in range(nb):
             cnt_pre[:, b] = row
             row = row + cnt_block[:, b]
 
     def prefix_pair(h):
-        return seq_copy(py_out.at[h], py_in.at[h], py_s.at[h], py_r.at[h], partner)
+        return seq_copy(py_out.at[h], py_in.at[h], py_s.at[0], py_r.at[h], partner)
 
     def prefix_hop(h, to):
-        return seq_copy(pz_out.at[h], pz_in.at[h], pz_s.at[h], pz_r.at[h], to)
+        return seq_copy(pz_out.at[h], pz_in.at[h], pz_s.at[0], pz_r.at[h], to)
 
     def prefix_back(h):
-        return seq_copy(pa_out.at[h], pa_in.at[h], pa_s.at[h], pa_r.at[h], partner)
+        return seq_copy(pa_out.at[h], pa_in.at[h], pa_s.at[0], pa_r.at[h], partner)
 
     loads[1].wait()
     loads[2].wait()
@@ -212,6 +246,10 @@
         return carry
 
     lax.fori_loop(0, heads, sums, 0)
+
+    @pl.when(jnp.logical_not(has_down))
+    def _():
+        take_counts()
 
     def make_keys(h, carry):
         book = cb_ref[h]
@@ -315,7 +353,11 @@
             relay(chunk)
 
     chain_at(0)
-    take_counts()
+
+    @pl.when(has_down)
+    def _():
+        take_counts()
+
     chain_at(1)
     loads[3].wait()
 
@@ -367,13 +409,13 @@
             code_acc[h] += code
 
     def later_pair(h):
-        return seq_copy(ly_out.at[h], ly_in.at[h], ly_s.at[h], ly_r.at[h], partner)
+        return seq_copy(ly_out.at[h], ly_in.at[h], ly_s.at[0], ly_r.at[h], partner)
 
     def later_hop(h, to):
-        return seq_copy(lz_out.at[h], lz_in.at[h], lz_s.at[h], lz_r.at[h], to)
+        return seq_copy(lz_out.at[h], lz_in.at[h], lz_s.at[0], lz_r.at[h], to)
 
     def later_back(h):
-        return seq_copy(la_out.at[h], la_in.at[h], la_s.at[h], la_r.at[h], partner)
+        return seq_copy(la_out.at[h], la_in.at[h], la_s.at[0], la_r.at[h], partner)
 
     def part_total(h, span):
         total = vpart[h, 0, span]
@@ -420,22 +462,22 @@
             later = later + vpart[h, b]
 
     def code_pair(h):
-        return seq_copy(cy_out.at[h], cy_in.at[h], cy_s.at[h], cy_r.at[h], partner)
+        return seq_copy(cy_out.at[h], cy_in.at[h], cy_s.at[0], cy_r.at[h], partner)
 
     def code_up(h, s):
-        return seq_copy(c_out.at[h, s], c_below.at[h, s], c_s.at[h, s], cb_r.at[h, s], me + 2)
+        return seq_copy(c_out.at[h, s], c_below.at[h, s], c_s.at[0], cb_r.at[h, s], me + 2)
 
     def code_down(h, s):
-        return seq_copy(c_out.at[h, s], c_above.at[h, s], c_s.at[h, s], cu_r.at[h, s], me - 2)
+        return seq_copy(c_out.at[h, s], c_above.at[h, s], c_s.at[0], cu_r.at[h, s], me - 2)
 
     def fin_up(h, s):
-        return seq_copy(c_fin.at[h, side, s], c_fin.at[h, side, s], fu_s.at[h, s], cf_r.at[h, s], me + 2)
+        return seq_copy(c_fin.at[side, h, s], c_fin.at[side, h, s], fu_s.at[0], cf_r.at[h, s], me + 2)
 
     def fin_down(h, s):
-        return seq_copy(c_fin.at[h, side, s], c_fin.at[h, side, s], fd_s.at[h, s], cf_r.at[h, s], me - 2)
+        return seq_copy(c_fin.at[side, h, s], c_fin.at[side, h, s], fd_s.at[0], cf_r.at[h, s], me - 2)
 
     def fin_pair(h, which, s):
-        return seq_copy(c_fin.at[h, which, s], c_fin.at[h, which, s], cp_s.at[h, s], cp_r.at[h, s], partner)
+        return seq_copy(c_fin.at[which, h, s], c_fin.at[which, h, s], cp_s.at[0], cp_r.at[h, s], partner)
 
     def send_code(h):
         cy_out[h] = code_acc[h, other_half].astype(BF16)
@@ -474,7 +516,7 @@
         for s in range(SUBS):
             @pl.when(at == center)
             def _(s=s):
-                c_fin[h, side, s] = c_out[h, s]
+                c_fin[side, h, s] = c_out[h, s]
 
             @pl.when(at != center)
             def _(s=s):
@@ -489,20 +531,23 @@
                 fin_up(h, s).start()
 
             fin_pair(h, side, s).start()
-            gc_ref[h, piece_of(side, s)] = c_fin[h, side, s].astype(F32)
+            gc_ref[h, piece_of(side, s)] = c_fin[side, h, s].astype(F32)
 
     def last_code(h):
         for s in range(SUBS):
             fin_pair(h, 1 - side, s).wait_recv()
-            gc_ref[h, piece_of(1 - side, s)] = c_fin[h, 1 - side, s].astype(F32)
+            gc_ref[h, piece_of(1 - side, s)] = c_fin[1 - side, h, s].astype(F32)
 
     for b in range(nb):
         final = b == nb - 1
         for part in range(parts):
             start = b * BLOCK + part * TILE
-            for chunk in range(start // CHUNK, (start + TILE) // CHUNK):
-                for slot in by_slot:
-                    arrive(slot, chunk)
+            for slot in by_slot:
+                if slot in feeds:
+                    for chunk in range(start // CHUNK, (start + TILE) // CHUNK):
+                        arrive(slot, chunk)
+                else:
+                    tile_copy(slot, start).wait_recv()
             project(start)
             if b == 0:
                 if part == 0:
@@ -560,6 +605,11 @@
 
     lax.fori_loop(0, heads, chain_step, 0)
 
+    @pl.when(soon & (behind > 0))
+    def _():
+        for h in range(heads):
+            later_back(h).start()
+
     def reduce_step(h, carry):
         reduce_code(h)
 
@@ -567,97 +617,90 @@
         def _():
             spread_code(h)
 
-        @pl.when(jnp.logical_not(soon) & has_down)
+        @pl.when(jnp.logical_not(soon) & has_down & (h == 1))
+        def _():
+            later_chain(h - 1)
+            later_back(h - 1).start()
+
+        return carry
+
+    lax.fori_loop(0, heads, reduce_step, 0)
+
+    def back_step(h, carry):
+        @pl.when(jnp.logical_not(soon | (has_down & (h == 0))))
         def _():
             later_chain(h)
+
+        @pl.when((behind == 0) | jnp.logical_not(soon | (has_down & (h == 0))))
+        def _():
             later_back(h).start()
 
         return carry
 
-    lax.fori_loop(0, heads, reduce_step, 0)
-
-    def back_step(h, carry):
-        @pl.when(jnp.logical_not(soon | has_down))
-        def _():
-            later_chain(h)
-
-        @pl.when(soon | jnp.logical_not(has_down))
-        def _():
-            later_back(h).start()
-
-        return carry
-
     lax.fori_loop(0, heads, back_step, 0)
 
-    def drain_early(h, carry):
-        prefix_pair(h).wait_send()
-        prefix_back(h).wait_send()
-
-        @pl.when(has_up)
-        def _():
-            prefix_hop(h, me + 2).wait_send()
-
-        return carry
-
-    lax.fori_loop(0, heads, drain_early, 0)
-
-    def drain_counts(to, carry):
-        count_copy(to, me).wait_send()
-        return carry
-
-    lax.fori_loop(me + 1, n_seq, drain_counts, 0)
-
-    for m, b in plan:
-        for chunk in range(chunks):
-            gather_copy(m, b, chunk).wait_send()
+    def sent(ref, sem):
+        return seq_copy(ref, ref, sem.at[0], sem.at[0], partner)
+
+    sent(py_out, py_s).wait_send()
+    sent(pa_out, pa_s).wait_send()
+
+    @pl.when(has_up)
+    def _():
+        sent(pz_out, pz_s).wait_send()
+
+    count_pair.wait_send()
+
+    @pl.when(has_up)
+    def _():
+        count_hop(me + 2).wait_send()
+
+    all_sent().wait_send()
+
+    quiet = (at == center) | jnp.logical_not(has_down & has_up)
 
     def spread_step(h, carry):
         @pl.when(at != center)
         def _():
             spread_code(h)
 
+        @pl.when(quiet)
+        def _():
+            later_gather(h)
+
         return carry
 
     lax.fori_loop(0, heads, spread_step, 0)
 
     def last_step(h, carry):
-        later_gather(h)
+        @pl.when(jnp.logical_not(quiet))
+        def _():
+            later_gather(h)
+
         last_code(h)
         return carry
 
     lax.fori_loop(0, heads, last_step, 0)
-
-    def drain(h, carry):
-        later_pair(h).wait_send()
-        later_back(h).wait_send()
-
-        @pl.when(has_down)
-        def _():
-            later_hop(h, me - 2).wait_send()
-
-        code_pair(h).wait_send()
-        for s in range(SUBS):
-            @pl.when(at < center)
-            def _(s=s):
-                code_up(h, s).wait_send()
-
-            @pl.when(at > center)
-            def _(s=s):
-                code_down(h, s).wait_send()
-
-            @pl.when((at <= center) & has_down)
-            def _(s=s):
-                fin_down(h, s).wait_send()
-
-            @pl.when((at >= center) & has_up)
-            def _(s=s):
-                fin_up(h, s).wait_send()
-
-            fin_pair(h, side, s).wait_send()
-
-        return carry
-
-    lax.fori_loop(0, heads, drain, 0)
+    sent(ly_out, ly_s).wait_send()
+    sent(la_out, la_s).wait_send()
+    sent(cy_out, cy_s).wait_send()
+    sent(c_fin.at[side], cp_s).wait_send()
+
+    @pl.when(has_down)
+    def _():
+        sent(lz_out, lz_s).wait_send()
+
+    @pl.when(at != center)
+    def _():
+        sent(c_out, c_s).wait_send()
+
+    @pl.when((at <= center) & has_down)
+    def _():
+        sent(c_fin.at[side], fd_s).wait_send()
+
+    @pl.when((at >= center) & has_up)
+    def _():
+        sent(c_fin.at[side], fu_s).wait_send()
 
 
 def write_out(*refs):
@@ -716,15 +759,18 @@
             pltpu.VMEM((heads, nb, entries, width), F32),
             pltpu.VMEM((heads, entries, width), F32),
             pltpu.VMEM((heads, entries, width), F32),
-            counts, pltpu.VMEM((n_seq, heads, 1, entries), F32),
+            counts, counts, counts, counts,
             halves, halves, halves, halves, halves, halves,
             halves, halves, halves, halves, halves, halves,
             halves, halves, pieces, pieces, pieces,
-            pltpu.VMEM((heads, 2, SUBS, half // SUBS, width), BF16),
-            dma((5,)), dma((chunks,)),
-            dma((n_head, chunks)), dma((n_head, chunks)),
-            dma((n_seq,)), dma((n_seq,)),
-        ] + [dma((heads,))] * 14 + [dma((heads, SUBS))] * 8,
+            pltpu.VMEM((2, heads, SUBS, half // SUBS, width), BF16),
+            dma((5,)), dma((2,)),
+            dma((1,)), dma((n_head // 2, row_count // TILE)), dma((max(n_head // 2 - 1, 1), chunks)),
+            dma((1,)), dma((1,)), dma((1,)), dma((1,)),
+        ] + [dma((1,)), dma((heads,))] * 7 + [
+            dma((1,)), dma((heads, SUBS)), dma((heads, SUBS)), dma((1,)), dma((heads, SUBS)),
+            dma((1,)), dma((1,)), dma((heads, SUBS)),
+        ],
         compiler_params=pltpu.CompilerParams(
             collective_id=0, has_side_effects=True, vmem_limit_bytes=50 * 1024 * 1024),
     )(*(pltpu.with_memory_space_constraint(x, pltpu.HBM) for x in (queries, values, codes.T, codebook, out_weight, grad_out)))

time: 67.2 us -> 65.6 us (0.976)
  Pallas kernels: 66.3 us -> 64.8 us
    pallas_call x1, Pallas kernels: 64.6 us -> 63.1 us  [per_device(): pl.pallas_call(functools.partial(kernel, n_seq, n_head), out_shape=(jax.S...]
where the time goes in v4:
time: 65.6 us; the launch traced here: 65.4 us
  Pallas kernels  64.8 us (99%)
    pallas_call x1, Pallas kernels, per_device(): pl.pallas_call(functools.partial(kernel, n_seq, n_head), out_shape=(jax.S...  63.1 us
    pallas_call x1, Pallas kernels, per_device(): pl.pallas_call(write_out, out_shape=tuple((jax.ShapeDtypeStruct(r.shape,...  1.69 us

profile of v4, /device:TPU:0, one launch (start us, length us, event | category | flops | bytes accessed | tf_op | source)
XLA Modules:
  0.0 65.4 jit_solution(11320392611322068344)
XLA Ops:
  0.6 63.1 %shard_map.85 = (bf16[1024,512]{1,0:T(8,128)(2,1)S(1)}, bf16[1024,512]{1,0:T(8,128)(2,1)S(1)}, f32[4,512,128]{2,1,0:T(8,128)S(1)}) custom-call(bf16[1024,512]{1,0:T(8,128)(2,1)} %q_in.1, bf16[1024,512]{1,0:T(8,128)(2,1)} %v_in.1, s32[4,1024]{1,0:T(4,128)} %bitcast.1, bf16[4,512,128]{2,1,0:T(8,128)(2,1)} %cb_in.1, bf16[512,2048]{1,0:T(8,128)(2,1)} %w_in.1, ...), custom_call_target="tpu_custom_call" | custom-call | tf_op jit(solution)/shard_map/pallas_call | solution.py:729
  63.7 1.7 %shard_map.86 = (bf16[1024,512]{1,0:T(8,128)(2,1)}, bf16[1024,512]{1,0:T(8,128)(2,1)}, f32[4,512,128]{2,1,0:T(8,128)}) custom-call(bf16[1024,512]{1,0:T(8,128)(2,1)S(1)} %get-tuple-element.6.refs_0_, bf16[1024,512]{1,0:T(8,128)(2,1)S(1)} %get-tuple-element.7.refs_1_, f32[4,512,128]{2,1,0:T(8,128)S(1)} %get-tuple-element.8.refs_2_), custom_call_target="tpu_custom_call" | custom-call | tf_op jit(solution)/shard_map/pallas_call | solution.py:777

commit v5 on v4

--- a/solution.py
+++ b/solution.py
@@ -556,7 +556,10 @@
         def values(h, carry, b=b, final=final):
             value_pass(h, b)
             if final:
-                send_later(h)
+                @pl.when(has_down)
+                def _():
+                    send_later(h)
+
             return carry
 
         lax.fori_loop(0, heads, values, 0)
@@ -581,20 +584,25 @@
             if final:
                 send_code(h)
 
-                @pl.when(jnp.logical_not(has_up) & (h >= 1))
+                @pl.when(jnp.logical_not(has_up))
                 def _():
-                    later_chain(h - 1)
+                    later_chain(h)
 
             return carry
 
         lax.fori_loop(0, heads, grads, 0)
+
+    def send_rest(h, carry):
+        @pl.when(jnp.logical_not(has_down))
+        def _():
+            send_later(h)
+
+        return carry
+
+    lax.fori_loop(0, heads, send_rest, 0)
 
     behind = outer - 1 - at
     soon = behind * 2 < outer
-
-    @pl.when(behind == 0)
-    def _():
-        later_chain(heads - 1)
 
     def chain_step(h, carry):
         @pl.when(soon & (behind > 0))

time: 65.6 us -> 65 us (level)
  Pallas kernels: 64.8 us -> 64.1 us
    pallas_call x1, Pallas kernels: 63.1 us -> 62.4 us  [per_device(): pl.pallas_call(functools.partial(kernel, n_seq, n_head), out_shape=(jax.S...]
where the time goes in v5:
time: 65 us; the launch traced here: 64.7 us
  Pallas kernels  64.1 us (99%)
    pallas_call x1, Pallas kernels, per_device(): pl.pallas_call(functools.partial(kernel, n_seq, n_head), out_shape=(jax.S...  62.4 us
    pallas_call x1, Pallas kernels, per_device(): pl.pallas_call(write_out, out_shape=tuple((jax.ShapeDtypeStruct(r.shape,...  1.69 us

profile of v5, /device:TPU:0, one launch (start us, length us, event | category | flops | bytes accessed | tf_op | source)
XLA Modules:
  0.0 64.7 jit_solution(14843374471033600261)
XLA Ops:
  0.6 62.4 %shard_map.85 = (bf16[1024,512]{1,0:T(8,128)(2,1)S(1)}, bf16[1024,512]{1,0:T(8,128)(2,1)S(1)}, f32[4,512,128]{2,1,0:T(8,128)S(1)}) custom-call(bf16[1024,512]{1,0:T(8,128)(2,1)} %q_in.1, bf16[1024,512]{1,0:T(8,128)(2,1)} %v_in.1, s32[4,1024]{1,0:T(4,128)} %bitcast.1, bf16[4,512,128]{2,1,0:T(8,128)(2,1)} %cb_in.1, bf16[512,2048]{1,0:T(8,128)(2,1)} %w_in.1, ...), custom_call_target="tpu_custom_call" | custom-call | tf_op jit(solution)/shard_map/pallas_call | solution.py:737
  63.0 1.7 %shard_map.86 = (bf16[1024,512]{1,0:T(8,128)(2,1)}, bf16[1024,512]{1,0:T(8,128)(2,1)}, f32[4,512,128]{2,1,0:T(8,128)}) custom-call(bf16[1024,512]{1,0:T(8,128)(2,1)S(1)} %get-tuple-element.6.refs_0_, bf16[1024,512]{1,0:T(8,128)(2,1)S(1)} %get-tuple-element.7.refs_1_, f32[4,512,128]{2,1,0:T(8,128)S(1)} %get-tuple-element.8.refs_2_), custom_call_target="tpu_custom_call" | custom-call | tf_op jit(solution)/shard_map/pallas_call | solution.py:785

commit v6 on v5

--- a/solution.py
+++ b/solution.py
@@ -11,6 +11,7 @@
 TILE = 256
 CHUNK = 128
 SUBS = 2
+WRITES = 4
 NEG = -1e30
 LOG2E = 1.4426950408889634
 F32 = jnp.float32
@@ -251,6 +252,42 @@
     def _():
         take_counts()
 
+    def prefix_chain(h):
+        prefix_pair(h).wait_recv()
+
+        @pl.when(jnp.logical_not(has_down))
+        def _():
+            pz_in[h] = jnp.zeros(pz_in.shape[1:], BF16)
+
+        @pl.when(has_down)
+        def _():
+            prefix_hop(h, me - 2).wait_recv()
+
+        below = pz_in[h].astype(F32)
+        pair = py_in[h].astype(F32)
+        total = own[h, 0, own_half]
+        for b in range(1, nb):
+            total += own[h, b, own_half]
+        pz_out[h] = (below + total + pair).astype(BF16)
+
+        @pl.when(has_up)
+        def _():
+            prefix_hop(h, me + 2).start()
+
+        pa_out[h] = (below + total * is_lo).astype(BF16)
+        prefix_back(h).start()
+        prefix = below + pair * is_hi
+        for b in range(nb):
+            cval[h, b, own_half] = prefix.astype(BF16)
+            prefix = prefix + own[h, b, own_half]
+
+    def prefix_gather(h):
+        prefix_back(h).wait_recv()
+        prefix = pa_in[h].astype(F32)
+        for b in range(nb):
+            cval[h, b, other_half] = prefix.astype(BF16)
+            prefix = prefix + own[h, b, other_half]
+
     def make_keys(h, carry):
         book = cb_ref[h]
         book_t[h] = jnp.transpose(book.astype(F32)).astype(BF16)
@@ -260,43 +297,17 @@
             keys_t[h, b] = jnp.transpose(key).astype(BF16)
         return carry
 
+    pairs = heads // 2
+
+    def chain_pair(j):
+        prefix_chain(2 * j)
+        prefix_chain(2 * j + 1)
+
+    @pl.when(jnp.logical_not(has_down))
+    def _():
+        chain_pair(0)
+
     lax.fori_loop(0, heads, make_keys, 0)
-
-    def prefix_chain(h):
-        prefix_pair(h).wait_recv()
-
-        @pl.when(jnp.logical_not(has_down))
-        def _():
-            pz_in[h] = jnp.zeros(pz_in.shape[1:], BF16)
-
-        @pl.when(has_down)
-        def _():
-            prefix_hop(h, me - 2).wait_recv()
-
-        below = pz_in[h].astype(F32)
-        pair = py_in[h].astype(F32)
-        total = own[h, 0, own_half]
-        for b in range(1, nb):
-            total += own[h, b, own_half]
-        pz_out[h] = (below + total + pair).astype(BF16)
-
-        @pl.when(has_up)
-        def _():
-            prefix_hop(h, me + 2).start()
-
-        pa_out[h] = (below + total * is_lo).astype(BF16)
-        prefix_back(h).start()
-        prefix = below + pair * is_hi
-        for b in range(nb):
-            cval[h, b, own_half] = prefix.astype(BF16)
-            prefix = prefix + own[h, b, own_half]
-
-    def prefix_gather(h):
-        prefix_back(h).wait_recv()
-        prefix = pa_in[h].astype(F32)
-        for b in range(nb):
-            cval[h, b, other_half] = prefix.astype(BF16)
-            prefix = prefix + own[h, b, other_half]
 
     def softmax(h, b):
         head_lanes = pl.ds(pl.multiple_of(h * width, width), width)
@@ -326,15 +337,6 @@
             cache_low[h, b, :, lanes] = (cache_exp * inverse).astype(BF16)
 
     rounds = heads * nb // 2
-    turn = 2 * at
-
-    def chain_at(slot):
-        h = slot - turn
-
-        @pl.when((h >= 0) & (h < heads))
-        def _():
-            prefix_chain(h)
-
     relay_at = {}
     for chunk in range(chunks):
         where = (0, 1, rounds - 1, "mid", "late", rounds, rounds + 2, rounds + heads - 1)[8 * chunk // chunks]
@@ -352,19 +354,26 @@
         for chunk in relay_at.get(name, []):
             relay(chunk)
 
-    chain_at(0)
+    @pl.when(jnp.logical_not(has_down))
+    def _():
+        for j in range(1, pairs):
+            chain_pair(j)
 
     @pl.when(has_down)
     def _():
         take_counts()
 
-    chain_at(1)
     loads[3].wait()
 
     def unit(k, carry):
         softmax(2 * k // nb, 2 * k % nb)
         softmax((2 * k + 1) // nb, (2 * k + 1) % nb)
-        chain_at(k + 2)
+        j = k - at + 1
+
+        @pl.when(has_down & (j >= 0) & (j < pairs))
+        def _():
+            chain_pair(j)
+
         relays(0, rounds, k)
         return carry
 
@@ -552,7 +561,6 @@
             if b == 0:
                 if part == 0:
                     relay_named("mid")
-                chain_at(rounds + 2 + part)
         def values(h, carry, b=b, final=final):
             value_pass(h, b)
             if final:
@@ -567,7 +575,7 @@
             relay_named("late")
 
             def rest(h, carry):
-                @pl.when(turn + h >= rounds + 2 + parts)
+                @pl.when(has_down & (at - 1 + h // 2 >= rounds))
                 def _():
                     prefix_chain(h)
 
@@ -713,7 +721,12 @@
 
 def write_out(*refs):
     sems = refs[-1]
-    copies = [pltpu.make_async_copy(refs[k], refs[k + 3], sems.at[k]) for k in range(3)]
+    copies = []
+    for k in range(3):
+        rows = refs[k].shape[0] // WRITES
+        for n in range(WRITES):
+            span = pl.ds(n * rows, rows)
+            copies.append(pltpu.make_async_copy(refs[k].at[span], refs[k + 3].at[span], sems.at[k, n]))
     for copy in copies:
         copy.start()
     for copy in copies:
@@ -787,7 +800,7 @@
         out_shape=tuple(jax.ShapeDtypeStruct(r.shape, r.dtype) for r in results),
         in_specs=[vmem] * 3,
         out_specs=(hbm,) * 3,
-        scratch_shapes=[dma((3,))],
+        scratch_shapes=[dma((3, WRITES))],
         compiler_params=pltpu.CompilerParams(vmem_limit_bytes=1024 * 1024),
     )(*results)
 

time: 65 us -> 66.4 us (1.022)
  Pallas kernels: 64.1 us -> 65.5 us
    pallas_call x1, Pallas kernels: 62.4 us -> 63.7 us  [per_device(): pl.pallas_call(functools.partial(kernel, n_seq, n_head), out_shape=(jax.S...]
where the time goes in v6:
time: 66.4 us; the launch traced here: 66.1 us
  Pallas kernels  65.5 us (99%)
    pallas_call x1, Pallas kernels, per_device(): pl.pallas_call(functools.partial(kernel, n_seq, n_head), out_shape=(jax.S...  63.7 us
    pallas_call x1, Pallas kernels, per_device(): pl.pallas_call(write_out, out_shape=tuple((jax.ShapeDtypeStruct(r.shape,...  1.76 us

profile of v6, /device:TPU:0, one launch (start us, length us, event | category | flops | bytes accessed | tf_op | source)
XLA Modules:
  0.0 66.1 jit_solution(3721766531227243054)
XLA Ops:
  0.6 63.7 %shard_map.85 = (bf16[1024,512]{1,0:T(8,128)(2,1)S(1)}, bf16[1024,512]{1,0:T(8,128)(2,1)S(1)}, f32[4,512,128]{2,1,0:T(8,128)S(1)}) custom-call(bf16[1024,512]{1,0:T(8,128)(2,1)} %q_in.1, bf16[1024,512]{1,0:T(8,128)(2,1)} %v_in.1, s32[4,1024]{1,0:T(4,128)} %bitcast.1, bf16[4,512,128]{2,1,0:T(8,128)(2,1)} %cb_in.1, bf16[512,2048]{1,0:T(8,128)(2,1)} %w_in.1, ...), custom_call_target="tpu_custom_call" | custom-call | tf_op jit(solution)/shard_map/pallas_call | solution.py:750
  64.4 1.8 %shard_map.86 = (bf16[1024,512]{1,0:T(8,128)(2,1)}, bf16[1024,512]{1,0:T(8,128)(2,1)}, f32[4,512,128]{2,1,0:T(8,128)}) custom-call(bf16[1024,512]{1,0:T(8,128)(2,1)S(1)} %get-tuple-element.6.refs_0_, bf16[1024,512]{1,0:T(8,128)(2,1)S(1)} %get-tuple-element.7.refs_1_, f32[4,512,128]{2,1,0:T(8,128)S(1)} %get-tuple-element.8.refs_2_), custom_call_target="tpu_custom_call" | custom-call | tf_op jit(solution)/shard_map/pallas_call | solution.py:798

commit v7 on v5

--- a/solution.py
+++ b/solution.py
@@ -531,6 +531,8 @@
                 fin_up(h, s).start()
 
             fin_pair(h, side, s).start()
+
+        for s in range(SUBS):
             gc_ref[h, piece_of(side, s)] = c_fin[side, h, s].astype(F32)
 
     def last_code(h):

time: 65 us -> 65 us (level)
  no operation moved by 1% of the time
where the time goes in v7:
time: 65 us; the launch traced here: 64.7 us
  Pallas kernels  64.1 us (99%)
    pallas_call x1, Pallas kernels, per_device(): pl.pallas_call(functools.partial(kernel, n_seq, n_head), out_shape=(jax.S...  62.4 us
    pallas_call x1, Pallas kernels, per_device(): pl.pallas_call(write_out, out_shape=tuple((jax.ShapeDtypeStruct(r.shape,...  1.69 us

profile of v7, /device:TPU:0, one launch (start us, length us, event | category | flops | bytes accessed | tf_op | source)
XLA Modules:
  0.0 64.7 jit_solution(17221696010790396623)
XLA Ops:
  0.6 62.4 %shard_map.85 = (bf16[1024,512]{1,0:T(8,128)(2,1)S(1)}, bf16[1024,512]{1,0:T(8,128)(2,1)S(1)}, f32[4,512,128]{2,1,0:T(8,128)S(1)}) custom-call(bf16[1024,512]{1,0:T(8,128)(2,1)} %q_in.1, bf16[1024,512]{1,0:T(8,128)(2,1)} %v_in.1, s32[4,1024]{1,0:T(4,128)} %bitcast.1, bf16[4,512,128]{2,1,0:T(8,128)(2,1)} %cb_in.1, bf16[512,2048]{1,0:T(8,128)(2,1)} %w_in.1, ...), custom_call_target="tpu_custom_call" | custom-call | tf_op jit(solution)/shard_map/pallas_call | solution.py:739
  63.0 1.7 %shard_map.86 = (bf16[1024,512]{1,0:T(8,128)(2,1)}, bf16[1024,512]{1,0:T(8,128)(2,1)}, f32[4,512,128]{2,1,0:T(8,128)}) custom-call(bf16[1024,512]{1,0:T(8,128)(2,1)S(1)} %get-tuple-element.6.refs_0_, bf16[1024,512]{1,0:T(8,128)(2,1)S(1)} %get-tuple-element.7.refs_1_, f32[4,512,128]{2,1,0:T(8,128)S(1)} %get-tuple-element.8.refs_2_), custom_call_target="tpu_custom_call" | custom-call | tf_op jit(solution)/shard_map/pallas_call | solution.py:787
